TPU v7x, 256 devices: a whole 4x4x8 slice. The times are simulated.
256 devices in a mesh: slab: 64 (over x, z, y_hi), grp: 4 (over y_lo, core).
Axes of the slice: x: 4, y: 4 (y_hi: 2, y_lo: 2; y = y_hi * 2 + y_lo), z: 8, core: 2. Of those that a mesh axis runs over, the one named last changes fastest.
Arguments:
- fine_input: bfloat16 [128, 128, 128, 128], P('slab', 'grp'), may hold values from -6 to 6
- out_grad: bfloat16 [128, 128, 128, 128], P('slab', 'grp')
- pre_norm: bfloat16 [256, 64, 4096], P('slab', None, 'grp')
- act_out: bfloat16 [256, 64, 4096], P('slab', None, 'grp'), as said below
- norm_gain: float32 [256], P('slab'), may hold values from 0.5 to 2
- w_down: bfloat16 [27, 128, 256], replicated, may hold values from -0.109375 to 0.109375
- w_up: bfloat16 [8, 256, 128], replicated, may hold values from -0.375 to 0.375
Outputs:
- grad_input: bfloat16 [128, 128, 128, 128], P('slab', 'grp')
- grad_down: float32 [256, 27, 128], P(('slab', 'grp'))
- grad_gain: float32 [256], P('slab')
- grad_shift: float32 [256], P('slab')
Inputs may be any that keep to these rules, and one draw needn't show every extreme that they name: `act_out`: the ReLU's output saved by the forward pass, zero where a unit was off.
All inputs are finite; a program needn't handle non-finite values.
Results may differ from a plain program's by a relative error of at most 0.0095.
Values may be sent and summed in bfloat16 or wider, within the bound.
A program may use at most 64 MiB of HBM per device.

v0:
```python
import math

import jax
import jax.numpy as jnp
from jax import lax
from jax.sharding import PartitionSpec as P

tap_places = ((1, 1), (0, 0), (1, 0))


def from_behind(shard, axis, by):
    devices = lax.axis_size(axis)
    pairs = [(i, i + by) for i in range(devices) if 0 <= i + by < devices]
    return lax.ppermute(shard, axis, pairs)


def norm_backward(
    values, grad_vals, saved_act, gain_vals, cell_total, reduce_moments, reduce_terms
):
    moment_one, moment_two = reduce_moments(
        jnp.sum(values, axis=(1, 2)), jnp.sum(values * values, axis=(1, 2))
    )
    channel_mean = moment_one / cell_total
    variance = moment_two / cell_total - channel_mean * channel_mean
    inv_std = lax.rsqrt(variance + 1e-05)
    normed = (values - channel_mean[:, None, None]) * inv_std[:, None, None]
    masked = jnp.where(saved_act > 0, grad_vals, jnp.zeros_like(grad_vals))
    total_one, total_two = reduce_terms(
        jnp.sum(masked, axis=(1, 2)), jnp.sum(masked * normed, axis=(1, 2))
    )
    shift_grad = total_one / cell_total
    gain_grad = total_two / cell_total
    grad_act = (
        (gain_vals * inv_std)[:, None, None]
        * (masked - shift_grad[:, None, None] - normed * gain_grad[:, None, None])
    ).astype(jnp.bfloat16)
    return (grad_act, gain_grad, shift_grad)


def local(fine_input, out_grad, pre_norm, act_out, norm_gain, w_down, w_up):
    fine_planes, fine_rows, fine_depth, width_in = fine_input.shape
    plane_count = fine_planes // 2
    row_count = fine_rows // 2
    depth = fine_depth // 2
    width_deep = w_up.shape[1]
    cell_count = plane_count * row_count * depth
    cell_total = pre_norm.shape[1] * pre_norm.shape[2] * lax.axis_size("grp")
    parity_grad = (
        out_grad.reshape(plane_count, 2, row_count, 2, depth, 2, width_in)
        .transpose(1, 3, 5, 0, 2, 4, 6)
        .reshape(8, cell_count, width_in)
    )
    deep_grad = jnp.einsum("poj,pnj->on", w_up, parity_grad, preferred_element_type=jnp.float32)
    deep_shape = (width_deep, plane_count, row_count * depth)
    deep_bf = deep_grad.astype(jnp.bfloat16).reshape(deep_shape)
    channel_grad = lax.all_to_all(deep_bf, "slab", split_axis=0, concat_axis=1, tiled=True)
    grad_channels, grad_gain, grad_shift = norm_backward(
        pre_norm.astype(jnp.float32),
        channel_grad.astype(jnp.float32),
        act_out,
        norm_gain,
        cell_total,
        lambda first_sum, second_sum: lax.psum((first_sum, second_sum), "grp"),
        lambda first_sum, second_sum: lax.psum((first_sum, second_sum), "grp"),
    )
    back_first = lax.all_to_all(grad_channels, "slab", split_axis=1, concat_axis=0, tiled=True)
    upper = from_behind(back_first, "slab", -1)
    with_plane = jnp.concatenate([back_first, upper], axis=1)
    row_data = from_behind(with_plane[:, :, :depth], "grp", -1)
    extended = jnp.concatenate([with_plane, row_data], axis=2)
    positions = lax.broadcasted_iota(jnp.int32, (1, 1, extended.shape[2]), 2) % depth
    tail_zero = jnp.zeros((width_deep, plane_count + 1, 1), jnp.bfloat16)
    shifted = jnp.where(
        positions != depth - 1,
        jnp.concatenate([extended[:, :, 1:], tail_zero], axis=2),
        jnp.zeros_like(extended),
    )
    fine_split = fine_input.reshape(plane_count, 2, row_count, 2, depth, 2, width_in)

    def window(sources, offsets):
        off_x, off_y, off_z = offsets
        source = sources[1] if off_z else sources[0]
        start_yz = off_y * depth
        return source[
            :, off_x : off_x + plane_count, start_yz : start_yz + row_count * depth
        ].reshape(source.shape[0], cell_count)

    tap_list = []
    for tap_index in range(27):
        par_x, off_x = tap_places[tap_index // 9]
        par_y, off_y = tap_places[tap_index // 3 % 3]
        par_z, off_z = tap_places[tap_index % 3]
        tap_list.append((tap_index, (par_x, par_y, par_z), (off_x, off_y, off_z)))
    fine_blocks = {}
    for par_x in range(2):
        for par_y in range(2):
            for par_z in range(2):
                fine_blocks[par_x, par_y, par_z] = fine_split[
                    :, par_x, :, par_y, :, par_z, :
                ].reshape(cell_count, width_in)
    blocks = {}
    for tap_index, parity, offsets in tap_list:
        term = jnp.einsum(
            "on,jo->nj",
            window((extended, shifted), offsets),
            w_down[tap_index],
            preferred_element_type=jnp.float32,
        )
        if parity in blocks:
            blocks[parity] = blocks[parity] + term
        else:
            blocks[parity] = term
    ordered = [
        blocks[par_x, par_y, par_z]
        for par_x in range(2)
        for par_y in range(2)
        for par_z in range(2)
    ]
    stacked = jnp.stack(ordered, 0).reshape(2, 2, 2, plane_count, row_count, depth, width_in)
    grad_input = (
        stacked.transpose(3, 0, 4, 1, 5, 2, 6)
        .reshape(fine_planes, fine_rows, fine_depth, width_in)
        .astype(jnp.bfloat16)
    )
    grad_scale = 1.0 / math.sqrt(cell_total)
    pieces = (extended, shifted)
    rows_out = [
        jnp.dot(window(pieces, offsets), fine_blocks[parity], preferred_element_type=jnp.float32)
        for tap_index, parity, offsets in tap_list
    ]
    grad_down = lax.psum_scatter(
        jnp.stack(rows_out, 1) * grad_scale, ("slab", "grp"), scatter_dimension=0, tiled=True
    )
    return (grad_input, grad_down, grad_gain, grad_shift)


def solution(mesh):
    return jax.shard_map(
        local,
        mesh=mesh,
        in_specs=(
            P("slab", "grp", None, None),
            P("slab", "grp", None, None),
            P("slab", None, "grp"),
            P("slab", None, "grp"),
            P("slab"),
            P(),
            P(),
        ),
        out_specs=(
            P("slab", "grp", None, None),
            P(("slab", "grp"), None, None),
            P("slab"),
            P("slab"),
        ),
        check_vma=False,
    )
```

profile of v0, /device:TPU:2, one launch (start us, length us, event | category | flops | bytes accessed | tf_op | source)
XLA Modules:
  0.0 406.9 jit_solution(15364128616952665557)
XLA Ops:
  7.2 2.2 copy.26
  9.4 0.7 fusion.1
  10.2 0.5 broadcast.58
  10.7 1.0 reduce
  11.7 1.1 reshape.138
  12.8 14.7 %all-to-all-start = ((bf16[64,2,2048]{2,1,0:T(2,128)(2,1)}), bf16[64,2,2048]{2,1,0:T(2,128)(2,1)S(1)}, u32[]{:S(2)}, u32[]{:S(2)}) async-start(bf16[64,2,2048]{2,1,0:T(2,128)(2,1)} %reshape.138), calls=%async_computation | async-start | bytes 1048576 | tf_op jit(solution)/shard_map/all_to_all | solution.py:56
  27.5 0.7 convert_reduce_fusion
  28.3 6.2 %all-reduce.3 = (f32[4]{0:T(128)S(1)}, f32[4]{0:T(128)S(1)}) all-reduce(f32[4]{0:T(128)S(1)} %get-tuple-element.7, f32[4]{0:T(128)S(1)} %get-tuple-element.6), channel_id=1, replica_groups=mesh['slab'=64,'grp'=4] {'grp'}, use_global_device_ids=true, to_apply=%region_1.0 | all-reduce | flops 8 | bytes 64 | tf_op jit(solution)/shard_map/psum | solution.py:63
  34.5 11.2 %all-to-all-done = bf16[64,2,2048]{2,1,0:T(2,128)(2,1)S(1)} async-done(((bf16[64,2,2048]{2,1,0:T(2,128)(2,1)}), bf16[64,2,2048]{2,1,0:T(2,128)(2,1)S(1)}, u32[]{:S(2)}, u32[]{:S(2)}) %all-to-all-start) | async-done | bytes 524320 | tf_op jit(solution)/shard_map/all_to_all | solution.py:56
  45.7 0.5 reshape.139
  46.2 1.1 bitcast_convert_fusion
  47.3 2.2 fusion.145
  49.6 5.7 %all-reduce.2 = (f32[4]{0:T(128)S(1)}, f32[4]{0:T(128)S(1)}) all-reduce(f32[4]{0:T(128)S(1)} %get-tuple-element.5, f32[4]{0:T(128)S(1)} %get-tuple-element.4), channel_id=1, replica_groups=mesh['slab'=64,'grp'=4] {'grp'}, use_global_device_ids=true, to_apply=%region_7.8 | all-reduce | flops 8 | bytes 64 | tf_op jit(solution)/shard_map/psum | solution.py:64
  55.3 1.8 fusion.64
  57.1 7.2 %all-to-all-start.1 = ((bf16[4,64,1024]{2,0,1:T(4,128)(2,1)}), bf16[4,64,1024]{2,0,1:T(4,128)(2,1)S(1)}, u32[]{:S(2)}, u32[]{:S(2)}) async-start(bf16[4,64,1024]{2,0,1:T(4,128)(2,1)} %fusion.64), calls=%async_computation.1 | async-start | bytes 1048576 | tf_op jit(solution)/shard_map/all_to_all | solution.py:66
  64.3 6.2 %fusion.147 = (bf16[1,1,16,1,64,1,128]{6,5,4,3,2,1,0:T(2,128)(2,1)S(1)}, bf16[1,1,16,1,64,1,128]{6,5,4,3,2,1,0:T(2,128)(2,1)S(1)}, bf16[1,1,16,1,64,1,128]{6,5,4...) fusion(bf16[1,2,16,2,64,2,128]{6,5,4,3,2,1,0:T(2,128)(2,1)} %bi, ...), kind=kLoop, calls=%fused_computation.214 | loop fusion | bytes 4194304 | tf_op jit(solution)/shard_map/slice | solution.py:98
  70.6 0.7 copy.33
  71.3 0.7 copy.34
  72.0 0.7 copy.35
  72.8 0.7 copy.36
  73.5 0.8 copy.37
  74.3 0.8 copy.38
  75.0 0.8 copy.39
  75.8 6.5 %all-to-all-done.1 = bf16[4,64,1024]{2,0,1:T(4,128)(2,1)S(1)} async-done(((bf16[4,64,1024]{2,0,1:T(4,128)(2,1)}), bf16[4,64,1024]{2,0,1:T(4,128)(2,1)S(1)}, u32[]{:S(2)}, u32[]{:S(2)}) %all-to-all-start.1) | async-done | bytes 524320 | tf_op jit(solution)/shard_map/all_to_all | solution.py:66
  82.6 1.9 fusion.27
  84.5 2.0 fusion.108
  86.5 3.8 collective-permute-start
  90.4 2.0 fusion.101
  92.4 2.0 fusion.91
  94.4 7.0 %collective-permute-done = bf16[256,1,1024]{2,0,1:T(8,128)(2,1)S(1)} collective-permute-done((bf16[256,1,1024]{2,0,1:T(8,128)(2,1)S(1)}, bf16[256,1,1024]{2,0,1:T(8,128)(2,1)S(1)}, u32[]{:S(2)}, u32[]{:S(2)}) %collective-permute-start) | collective-permute-done | bytes 524320 | tf_op jit(solution)/shard_map/ppermute | solution.py:14
  101.4 1.5 collective-permute-start.1
  102.9 2.0 fusion.73
  104.9 0.8 fusion.13
  106.0 2.2 fusion.77
  108.2 2.2 fusion.78
  110.3 2.0 fusion.81
  112.3 2.0 fusion.80
  114.3 2.2 fusion.79
  116.5 2.0 fusion.82
  118.5 0.4 fusion.56
  118.9 0.7 fusion.67
  122.1 0.4 fusion.47
  124.8 0.4 fusion.38
  127.5 2.0 broadcast_multiply_fusion
  129.6 1.6 convolution_add_fusion.8
  131.2 1.3 convolution_add_fusion.7
  132.6 0.4 convolution_add_fusion.12
  133.0 0.3 convolution_add_fusion.11
  133.3 0.6 fusion.25
  134.0 0.4 fusion.23
  134.4 0.4 fusion.21
  134.8 0.4 fusion.19
  135.3 0.4 fusion.17
  135.7 0.3 fusion.93
  136.1 0.4 convolution_add_fusion.4
  136.4 0.3 convolution_add_fusion.3
  136.8 0.4 fusion.3
  137.2 0.3 copy-done.18
  137.5 0.4 fusion.2
  138.0 0.4 fusion.29
  138.5 0.4 fusion.15
  138.9 3.5 copy.29
  142.3 256.3 %all-reduce.6.cloned.1.call-done = f32[256,27,128]{2,0,1:T(8,128)} async-done(((f32[256,27,128]{2,0,1:T(8,128)}), f32[256,27,128]{2,0,1:T(8,128)}) %all-reduce.6.cloned.1.call-update) | async-done | bytes 3538960
  398.6 1.5 constant_dynamic-slice_fusion
  (88 shorter events, 7.9 us)
Async XLA Ops:
  7.2 2.2 copy-start
  10.1 17.4 %copy-start.4 = (bf16[4,64,1024]{2,1,0:T(8,128)(2,1)S(1)}, bf16[4,64,1024]{2,1,0:T(8,128)(2,1)}, u32[]{:S(2)}) copy-start(bf16[4,64,1024]{2,1,0:T(8,128)(2,1)} %param.9) | copy-start | bytes 1572868
  10.1 24.3 %copy-start.25 = (f32[4]{0:T(128)S(1)}, f32[4]{0:T(128)}, u32[]{:S(2)}) copy-start(f32[4]{0:T(128)} %param.11) | copy-start | bytes 52
  12.8 32.9 %all-to-all-start = ((bf16[64,2,2048]{2,1,0:T(2,128)(2,1)}), bf16[64,2,2048]{2,1,0:T(2,128)(2,1)S(1)}, u32[]{:S(2)}, u32[]{:S(2)}) async-start(bf16[64,2,2048]{2,1,0:T(2,128)(2,1)} %reshape.138), calls=%async_computation | async-start | bytes 1048576 | tf_op jit(solution)/shard_map/all_to_all | solution.py:56
  47.3 7.9 %copy-start.9 = (bf16[4,64,1024]{2,1,0:T(8,128)(2,1)S(1)}, bf16[4,64,1024]{2,1,0:T(8,128)(2,1)}, u32[]{:S(2)}) copy-start(bf16[4,64,1024]{2,1,0:T(8,128)(2,1)} %param.10) | copy-start | bytes 1572868
  55.3 15.2 %copy-start.23 = (f32[4]{0:T(128)}, f32[4]{0:T(128)S(1)}, u32[]{:S(2)}) copy-start(f32[4]{0:T(128)S(1)} %get-tuple-element.25) | copy-start | bytes 52
  55.3 15.2 %copy-start.24 = (f32[4]{0:T(128)}, f32[4]{0:T(128)S(1)}, u32[]{:S(2)}) copy-start(f32[4]{0:T(128)S(1)} %get-tuple-element.26) | copy-start | bytes 52
  57.1 25.3 %all-to-all-start.1 = ((bf16[4,64,1024]{2,0,1:T(4,128)(2,1)}), bf16[4,64,1024]{2,0,1:T(4,128)(2,1)S(1)}, u32[]{:S(2)}, u32[]{:S(2)}) async-start(bf16[4,64,1024]{2,0,1:T(4,128)(2,1)} %fusion.64), calls=%async_computation.1 | async-start | bytes 1048576 | tf_op jit(solution)/shard_map/all_to_all | solution.py:66
  64.3 334.3 %all-reduce.6.cloned.1.call-start = ((), (), s32[]{:S(2)}) async-start(), calls=%async_computation.2 | async-start | bytes 7077888
  86.5 14.8 %collective-permute-start = (bf16[256,1,1024]{2,0,1:T(8,128)(2,1)S(1)}, bf16[256,1,1024]{2,0,1:T(8,128)(2,1)S(1)}, u32[]{:S(2)}, u32[]{:S(2)}) collective-permute-start(bf16[256,1,1024]{2,0,1:T(8,128)(2,1)S(1)} %all_to_all.24), channel_id=1, source_target_pairs={{4,0},{8,4},{12,8},{16,12},{20,16},{24,20},{28,24},{32,28},{36,32}... | collective-permute-start | bytes 1572872 | tf_op jit(solution)/shard_map/ppermute | solution.py:14
  101.4 3.5 collective-permute-start.1
  116.5 3.2 copy-start.3
  118.9 1.4 copy-start.5
  118.9 1.7 copy-start.6
  119.7 1.5 copy-start.1
  120.9 1.2 copy-start.7
  121.2 1.3 copy-start.8
  121.8 1.3 copy-start.21
  122.1 1.3 copy-start.22
  129.6 3.0 copy-start.13
  129.6 3.0 copy-start.20
  131.2 2.1 copy-start.14
  131.2 2.1 copy-start.17
  132.6 1.4 copy-start.15
  133.3 1.5 copy-start.16
  134.8 1.2 copy-start.2
  134.8 1.2 copy-start.12
  135.7 1.1 copy-start.19
  136.4 1.1 copy-start.18
  136.8 1.1 copy-start.10
  136.8 1.2 copy-start.11
Sparse Core Ops, SparseCore 0:
  129.7 268.8 all-reduce.5
where the time goes:
time: 408 us; the launch traced here: 407 us
  waiting for transfers between devices  281 us (69%)
  matrix products  39.7 us (10%)
  starting transfers between devices  27.1 us (7%)
  local copies, waits for them, and re-layouts  21.7 us (5%)
  between operations  14.8 us (4%)
  blocking collectives  11.9 us (3%)
  other arithmetic  10.7 us (3%)
    unnamed x2, waiting for transfers between devices  256 us
    dot_general x27, matrix products, local(): jnp.einsum('on,jo->nj', window((extended, shifted), offsets), w_down[tap_...  31 us
    all_to_all x1, starting transfers between devices, local(): lax.all_to_all(deep_bf, 'slab', split_axis=0, concat_axis=1, tiled=True)  14.7 us
    psum x2, blocking collectives, local(): lax.psum((first_sum, second_sum), 'grp')  11.9 us
    all_to_all x1, waiting for transfers between devices, local(): lax.all_to_all(deep_bf, 'slab', split_axis=0, concat_axis=1, tiled=True)  11.2 us
    unnamed x64, local copies, waits for them, and re-layouts  9.06 us
  transfers between devices with their start and end apart: 5, of which 4 were waited for; matrix products, arithmetic and copies ran while one was open for 7% of the time, Pallas kernels for 0%

commit v1 on v0

--- a/solution.py
+++ b/solution.py
@@ -1,9 +1,164 @@
+import functools
 import math
 
 import jax
 import jax.numpy as jnp
 from jax import lax
+from jax.experimental import pallas as pl
+from jax.experimental.pallas import tpu as pltpu
 from jax.sharding import PartitionSpec as P
+
+MESH = pl.DeviceIdType.MESH
+
+
+def place():
+    slab = lax.axis_index("slab")
+    grp = lax.axis_index("grp")
+    return slab // 16, (slab % 2) * 2 + grp // 2, slab // 2 % 8, grp % 2
+
+
+def device(x, y, z, core):
+    return (x * 16 + z * 2 + y // 2, y % 2 * 2 + core)
+
+
+def remote(src, dst, send, recv, where):
+    return pltpu.make_async_remote_copy(
+        src_ref=src, dst_ref=dst, send_sem=send, recv_sem=recv, device_id=where, device_id_type=MESH
+    )
+
+
+FIRST = 14
+
+
+def rs_peers(x, y, z, core):
+    peers = [device(x, y, z, 1 - core)]
+    peers += [device((x + d) % 4, y, z, core) for d in (1, 2, 3)]
+    peers += [device(x, (y + d) % 4, z, core) for d in (1, 2, 3)]
+    peers += [device(x, y, (z + d) % 8, core) for d in range(1, 8)]
+    return peers
+
+
+def rs_kernel(scale, q_ref, out_ref, pair_out, pair_in, ax, ax_in, by, by_in, ay, ay_in, bx, bx_in,
+              zz, zs, zs_in, send_sem, recv_sem):
+    x, y, z, core = place()
+    barrier = pltpu.get_barrier_semaphore()
+    peers = rs_peers(x, y, z, core)
+    for peer in peers:
+        pl.semaphore_signal(barrier, inc=1, device_id=peer, device_id_type=MESH)
+
+    def pack(tap, carry):
+        pair_out[tap] = q_ref[tap, 1 - core].astype(jnp.bfloat16)
+        return carry
+
+    lax.fori_loop(0, 27, pack, 0)
+    pl.semaphore_wait(barrier, len(peers))
+    pair = remote(pair_out, pair_in, send_sem.at[0], recv_sem.at[0], peers[0])
+    pair.start()
+    pair.wait()
+
+    def split_first(tap, carry):
+        total = q_ref[tap, core] + pair_in[tap].astype(jnp.float32)
+        for block in range(4):
+            ax[block, tap] = total[:, block].astype(jnp.bfloat16)
+        return carry
+
+    def split_last(tap, carry):
+        total = q_ref[tap + FIRST, core] + pair_in[tap + FIRST].astype(jnp.float32)
+        for block in range(4):
+            by[block, tap] = total[block].astype(jnp.bfloat16)
+        return carry
+
+    lax.fori_loop(0, FIRST, split_first, 0)
+    wave = []
+    for d in (1, 2, 3):
+        wave.append(remote(ax.at[(x + d) % 4], ax_in.at[d - 1], send_sem.at[d], recv_sem.at[d], peers[d]))
+        wave[-1].start()
+    lax.fori_loop(0, 27 - FIRST, split_last, 0)
+    for d in (1, 2, 3):
+        wave.append(remote(by.at[(y + d) % 4], by_in.at[d - 1], send_sem.at[3 + d], recv_sem.at[3 + d], peers[3 + d]))
+        wave[-1].start()
+    for copy in wave[:3]:
+        copy.wait()
+
+    def add_ax(tap, carry):
+        total = ax[x, tap].astype(jnp.float32)
+        for d in range(3):
+            total = total + ax_in[d, tap].astype(jnp.float32)
+        for block in range(4):
+            ay[block, tap] = total[block]
+        return carry
+
+    lax.fori_loop(0, FIRST, add_ax, 0)
+    later = []
+    for d in (1, 2, 3):
+        later.append(remote(ay.at[(y + d) % 4], ay_in.at[d - 1], send_sem.at[6 + d], recv_sem.at[6 + d], peers[3 + d]))
+        later[-1].start()
+    for copy in wave[3:]:
+        copy.wait()
+
+    def add_by(tap, carry):
+        total = by[y, tap].astype(jnp.float32)
+        for d in range(3):
+            total = total + by_in[d, tap].astype(jnp.float32)
+        for block in range(4):
+            bx[block, tap] = total[block]
+        return carry
+
+    lax.fori_loop(0, 27 - FIRST, add_by, 0)
+    for d in (1, 2, 3):
+        later.append(remote(bx.at[(x + d) % 4], bx_in.at[d - 1], send_sem.at[9 + d], recv_sem.at[9 + d], peers[d]))
+        later[-1].start()
+    for copy in later:
+        copy.wait()
+    for tap in range(27):
+        if tap < FIRST:
+            total = ay[y, tap] + ay_in[0, tap] + ay_in[1, tap] + ay_in[2, tap]
+        else:
+            t = tap - FIRST
+            total = bx[x, t] + bx_in[0, t] + bx_in[1, t] + bx_in[2, t]
+        zz[tap * 8 : tap * 8 + 8, :] = total
+    for row in range(8):
+        zs[row] = zz[pl.ds(row, 27, stride=8), :]
+    last = []
+    for d in range(1, 8):
+        last.append(remote(zs.at[(z + d) % 8], zs_in.at[d - 1], send_sem.at[12 + d], recv_sem.at[12 + d], peers[6 + d]))
+        last[-1].start()
+    for copy in last:
+        copy.wait()
+    total = zs[z]
+    for d in range(7):
+        total = total + zs_in[d]
+    out_ref[...] = total * scale
+
+
+def reduce_scatter(q, scale):
+    bf, f32 = jnp.bfloat16, jnp.float32
+    rest = 27 - FIRST
+    return pl.pallas_call(
+        functools.partial(rs_kernel, scale),
+        out_shape=jax.ShapeDtypeStruct((27, 128), f32),
+        in_specs=[pl.BlockSpec(memory_space=pltpu.VMEM)],
+        out_specs=pl.BlockSpec(memory_space=pltpu.VMEM),
+        scratch_shapes=[
+            pltpu.VMEM((27, 4, 4, 8, 128), bf),
+            pltpu.VMEM((27, 4, 4, 8, 128), bf),
+            pltpu.VMEM((4, FIRST, 4, 8, 128), bf),
+            pltpu.VMEM((3, FIRST, 4, 8, 128), bf),
+            pltpu.VMEM((4, rest, 4, 8, 128), bf),
+            pltpu.VMEM((3, rest, 4, 8, 128), bf),
+            pltpu.VMEM((4, FIRST, 8, 128), f32),
+            pltpu.VMEM((3, FIRST, 8, 128), f32),
+            pltpu.VMEM((4, rest, 8, 128), f32),
+            pltpu.VMEM((3, rest, 8, 128), f32),
+            pltpu.VMEM((216, 128), f32),
+            pltpu.VMEM((8, 27, 128), f32),
+            pltpu.VMEM((7, 27, 128), f32),
+            pltpu.SemaphoreType.DMA((20,)),
+            pltpu.SemaphoreType.DMA((20,)),
+        ],
+        compiler_params=pltpu.CompilerParams(collective_id=0, has_side_effects=True),
+    )(q)
+
 
 tap_places = ((1, 1), (0, 0), (1, 0))
 
@@ -123,14 +278,19 @@
         .astype(jnp.bfloat16)
     )
     grad_scale = 1.0 / math.sqrt(cell_total)
-    pieces = (extended, shifted)
+    pieces = [
+        piece.reshape(4, 8, 2, 2, 2, *piece.shape[1:])
+        .transpose(4, 2, 3, 0, 1, 5, 6)
+        .reshape(piece.shape)
+        for piece in (extended, shifted)
+    ]
     rows_out = [
         jnp.dot(window(pieces, offsets), fine_blocks[parity], preferred_element_type=jnp.float32)
         for tap_index, parity, offsets in tap_list
     ]
-    grad_down = lax.psum_scatter(
-        jnp.stack(rows_out, 1) * grad_scale, ("slab", "grp"), scatter_dimension=0, tiled=True
-    )
+    grad_down = reduce_scatter(
+        jnp.stack(rows_out, 0).reshape(27, 2, 4, 4, 8, width_in), grad_scale
+    )[None]
     return (grad_input, grad_down, grad_gain, grad_shift)
 
 

time: 408 us -> 174 us (0.43)
  waiting for transfers between devices: 281 us -> 33.4 us
  Pallas kernels: 0 us -> 29.4 us
  between operations: 14.8 us -> 1.17 us
    unnamed x2 -> x0, waiting for transfers between devices: 256 us -> none
    pallas_call x0 -> x1, Pallas kernels: none -> 29.4 us  [reduce_scatter(): pl.pallas_call(functools.partial(rs_kernel, scale), out_shape=jax.ShapeDt...]
    dot_general x27, matrix products: 31 us -> 13 us  [local(): jnp.einsum('on,jo->nj', window((extended, shifted), offsets), w_down[tap_...]
    dot_general x27, matrix products: 7.94 us -> 25.9 us  [local(): jnp.dot(window(pieces, offsets), fine_blocks[parity], preferred_element_t...]
    unnamed x64 -> x30, local copies, waits for them, and re-layouts: 9.06 us -> 4.11 us
    ppermute x2, waiting for transfers between devices: 6.97 us -> 11.9 us  [from_behind(): return lax.ppermute(shard, axis, pairs)]
  transfers between devices with their start and end apart: 5 -> 4, of which waited for: 4 -> 4; matrix products, arithmetic and copies ran while one was open for 7% -> 5% of each run, Pallas kernels for 0% -> 0%
where the time goes in v1:
time: 174 us; the launch traced here: 173 us
  matrix products  39.6 us (23%)
  waiting for transfers between devices  33.4 us (19%)
  Pallas kernels  29.4 us (17%)
  starting transfers between devices  27.1 us (16%)
  local copies, waits for them, and re-layouts  22.3 us (13%)
  blocking collectives  11.9 us (7%)
  other arithmetic  8.31 us (5%)
    pallas_call x1, Pallas kernels, reduce_scatter(): pl.pallas_call(functools.partial(rs_kernel, scale), out_shape=jax.ShapeDt...  29.4 us
    dot_general x27, matrix products, local(): jnp.dot(window(pieces, offsets), fine_blocks[parity], preferred_element_t...  25.9 us
    all_to_all x1, starting transfers between devices, local(): lax.all_to_all(deep_bf, 'slab', split_axis=0, concat_axis=1, tiled=True)  14.7 us
    dot_general x27, matrix products, local(): jnp.einsum('on,jo->nj', window((extended, shifted), offsets), w_down[tap_...  13 us
    psum x2, blocking collectives, local(): lax.psum((first_sum, second_sum), 'grp')  11.9 us
    ppermute x2, waiting for transfers between devices, from_behind(): return lax.ppermute(shard, axis, pairs)  11.9 us
    all_to_all x1, waiting for transfers between devices, local(): lax.all_to_all(deep_bf, 'slab', split_axis=0, concat_axis=1, tiled=True)  11.2 us
    all_to_all x1, waiting for transfers between devices, local(): lax.all_to_all(grad_channels, 'slab', split_axis=1, concat_axis=0, tiled=...  10.3 us
  transfers between devices with their start and end apart: 4, of which 4 were waited for; matrix products, arithmetic and copies ran while one was open for 5% of the time, Pallas kernels for 0%

profile of v1, /device:TPU:2, one launch (start us, length us, event | category | flops | bytes accessed | tf_op | source)
XLA Modules:
  0.0 173.1 jit_solution(2608585555599040503)
XLA Ops:
  0.6 2.2 %copy.59 = bf16[2,2,2,1,16,64,128]{6,5,4,2,1,0,3:T(8,128)(2,1)S(1)} copy(bf16[2,2,2,1,16,64,128]{6,2,5,1,4,0,3:T(2,128)(2,1)} %bitcast.474) | data formatting | bytes 4194304 | tf_op jit(solution)/shard_map/transpose | solution.py:205
  2.8 0.7 fusion.1
  4.1 1.0 reduce
  5.2 1.1 reshape.374
  6.3 14.7 %all-to-all-start = ((bf16[64,2,2048]{2,1,0:T(2,128)(2,1)}), bf16[64,2,2048]{2,1,0:T(2,128)(2,1)S(1)}, u32[]{:S(2)}, u32[]{:S(2)}) async-start(bf16[64,2,2048]{2,1,0:T(2,128)(2,1)} %reshape.374), calls=%async_computation | async-start | bytes 1048576 | tf_op jit(solution)/shard_map/all_to_all | solution.py:211
  21.0 0.7 convert_reduce_fusion
  21.7 6.2 %all-reduce.2 = (f32[4]{0:T(128)S(1)}, f32[4]{0:T(128)S(1)}) all-reduce(f32[4]{0:T(128)S(1)} %get-tuple-element.23, f32[4]{0:T(128)S(1)} %get-tuple-element.22), channel_id=1, replica_groups=mesh['slab'=64,'grp'=4] {'grp'}, use_global_device_ids=true, to_apply=%region_1.0 | all-reduce | flops 8 | bytes 64 | tf_op jit(solution)/shard_map/psum | solution.py:218
  27.9 11.2 %all-to-all-done = bf16[64,2,2048]{2,1,0:T(2,128)(2,1)S(1)} async-done(((bf16[64,2,2048]{2,1,0:T(2,128)(2,1)}), bf16[64,2,2048]{2,1,0:T(2,128)(2,1)S(1)}, u32[]{:S(2)}, u32[]{:S(2)}) %all-to-all-start) | async-done | bytes 524320 | tf_op jit(solution)/shard_map/all_to_all | solution.py:211
  39.2 0.5 reshape.375
  39.7 1.1 bitcast_convert_fusion
  40.8 2.2 %fusion.144 = (f32[4]{0:T(128)S(1)}, f32[4]{0:T(128)S(1)}) fusion(f32[64,4,1,1024]{3,2,1,0:T(1,128)S(1)} %bitcast_convert_fusion, bf16[4,64,1024]{2,1,0:T(8,128)(2,1)} %param.10, f32[4]{0:T(128)S(1)} %get-tuple-element.29, f32[4]{0:T(128)S(1)} %get-tuple-element.46, bf16[4,64,1024]{2,1,0:T(8,128)(2,1)S(1)} %copy-done.1), kind=kLoop, calls=%fused_computation.209 | loop fusion | flops 2097144 | bytes 2097216 | tf_op jit(solution)/shard_map/reduce_sum | solution.py:184
  43.1 5.7 %all-reduce.1 = (f32[4]{0:T(128)S(1)}, f32[4]{0:T(128)S(1)}) all-reduce(f32[4]{0:T(128)S(1)} %get-tuple-element.21, f32[4]{0:T(128)S(1)} %get-tuple-element.20), channel_id=1, replica_groups=mesh['slab'=64,'grp'=4] {'grp'}, use_global_device_ids=true, to_apply=%region_7.8 | all-reduce | flops 8 | bytes 64 | tf_op jit(solution)/shard_map/psum | solution.py:219
  48.8 1.8 %fusion.64 = bf16[4,64,1024]{2,0,1:T(4,128)(2,1)} fusion(f32[4]{0:T(128)S(1)} %get-tuple-element.47, f32[4]{0:T(128)S(1)} %get-tuple-element.29, f32[4]{0:T(128)S(1)} %get-tuple-element.46, f32[4]{0:T(128)S(1)} %get-tuple-element.48, f32[4]{0:T(128)S(1)} %get-tuple-element.28, bf16[4,64,1024]{2,1,0:T(8,128)(2,1)S(1)} %copy-done.1, ...), kind=kLoop, calls=%fused_computation.116 | loop fusion | flops 2621440 | bytes 2621520 | tf_op jit(solution)/shard_map/convert_element_type | solution.py:191
  50.6 7.2 %all-to-all-start.1 = ((bf16[4,64,1024]{2,0,1:T(4,128)(2,1)}), bf16[4,64,1024]{2,0,1:T(4,128)(2,1)S(1)}, u32[]{:S(2)}, u32[]{:S(2)}) async-start(bf16[4,64,1024]{2,0,1:T(4,128)(2,1)} %fusion.64), calls=%async_computation.1 | async-start | bytes 1048576 | tf_op jit(solution)/shard_map/all_to_all | solution.py:221
  57.8 6.6 %fusion.146 = (bf16[1,1,16,1,64,1,128]{6,5,4,3,2,1,0:T(2,128)(2,1)S(1)}, bf16[1,1,16,1,64,1,128]{6,5,4,3,2,1,0:T(2,128)(2,1)S(1)}, bf16[1,1,16,1,64,1,128]{6,5,4...) fusion(bf16[1,2,16,2,64,2,128]{6,5,4,3,2,1,0:T(2,128)(2,1)} %bi, ...), kind=kLoop, calls=%fused_computation.211 | loop fusion | bytes 4194304 | tf_op jit(solution)/shard_map/slice | solution.py:253
  64.4 0.8 copy.91
  65.5 10.3 %all-to-all-done.1 = bf16[4,64,1024]{2,0,1:T(4,128)(2,1)S(1)} async-done(((bf16[4,64,1024]{2,0,1:T(4,128)(2,1)}), bf16[4,64,1024]{2,0,1:T(4,128)(2,1)S(1)}, u32[]{:S(2)}, u32[]{:S(2)}) %all-to-all-start.1) | async-done | bytes 524320 | tf_op jit(solution)/shard_map/all_to_all | solution.py:221
  75.9 0.9 all_to_all.24
  76.9 1.3 fusion.88
  78.2 1.2 fusion.27
  79.4 3.8 %collective-permute-start = (bf16[256,1,1024]{2,0,1:T(8,128)(2,1)}, bf16[256,1,1024]{2,0,1:T(8,128)(2,1)S(1)}, u32[]{:S(2)}, u32[]{:S(2)}) collective-permute-start(bf16[256,1,1024]{2,0,1:T(8,128)(2,1)} %all_to_all.24), channel_id=1, source_target_pairs={{4,0},{8,4},{12,8},{16,12},{20,16},{24,20},{28,24},{32,28},{36,32}... | collective-permute-start | bytes 1572872 | tf_op jit(solution)/shard_map/ppermute | solution.py:169
  84.0 10.5 %collective-permute-done = bf16[256,1,1024]{2,0,1:T(8,128)(2,1)S(1)} collective-permute-done((bf16[256,1,1024]{2,0,1:T(8,128)(2,1)}, bf16[256,1,1024]{2,0,1:T(8,128)(2,1)S(1)}, u32[]{:S(2)}, u32[]{:S(2)}) %collective-permute-start) | collective-permute-done | bytes 524320 | tf_op jit(solution)/shard_map/ppermute | solution.py:169
  94.5 1.5 collective-permute-start.1
  96.4 1.4 collective-permute-done.1
  97.8 0.8 fusion.13
  99.1 0.5 fusion.75
  99.7 0.6 fusion.69
  100.6 0.5 fusion.76
  101.5 1.2 copy.63
  103.4 0.6 convolution_add_fusion.4
  106.0 0.7 fusion.148
  106.8 1.2 copy.66
  108.3 0.7 fusion.147
  111.8 0.8 fusion.29
  113.1 3.5 %copy.62 = bf16[1,2,16,2,64,2,128]{6,5,4,3,2,1,0:T(2,128)(2,1)} copy(bf16[1,2,16,2,64,2,128]{6,4,2,5,3,1,0:T(8,128)(2,1)S(1)} %bitcast.476) | data formatting | bytes 4194304 | tf_op jit(solution)/shard_map/convert_element_type | solution.py:278
  116.6 1.0 fusion.56
  117.5 0.9 fusion.55
  118.5 1.0 fusion.54
  119.4 1.0 fusion.53
  120.4 0.9 fusion.52
  121.3 1.0 fusion.51
  122.3 1.0 fusion.50
  123.2 1.0 fusion.49
  124.2 1.0 fusion.48
  125.2 0.9 fusion.47
  126.1 1.0 fusion.46
  127.1 1.0 fusion.45
  128.0 1.0 fusion.44
  129.0 1.0 fusion.43
  130.0 1.0 fusion.42
  130.9 1.0 fusion.41
  131.9 1.0 fusion.40
  132.8 1.0 fusion.39
  133.8 1.0 fusion.38
  134.8 0.9 fusion.37
  135.7 0.9 fusion.36
  136.7 1.0 fusion.35
  137.6 1.0 fusion.34
  138.6 1.0 fusion.33
  139.6 1.0 fusion.32
  140.5 1.0 fusion.31
  141.5 1.0 fusion.30.q_ref
  142.4 29.4 %shard_map.102 = f32[27,128]{1,0:T(8,128)} custom-call(f32[27,2,4,4,8,128]{5,4,3,2,1,0:T(8,128)} %fusion.30.q_ref), custom_call_target="tpu_custom_call" | custom-call | tf_op jit(solution)/shard_map/pallas_call | solution.py:137
  171.8 1.3 copy.75
  (58 shorter events, 9.5 us)
Async XLA Ops:
  0.6 2.2 %copy-start = (bf16[8,256,128]{2,1,0:T(8,128)(2,1)S(1)}, bf16[8,256,128]{2,1,0:T(8,128)(2,1)}, u32[]{:S(2)}) copy-start(bf16[8,256,128]{2,1,0:T(8,128)(2,1)} %param.13) | copy-start | bytes 1572868
  3.6 17.4 %copy-start.1 = (bf16[4,64,1024]{2,1,0:T(8,128)(2,1)S(1)}, bf16[4,64,1024]{2,1,0:T(8,128)(2,1)}, u32[]{:S(2)}) copy-start(bf16[4,64,1024]{2,1,0:T(8,128)(2,1)} %param.9) | copy-start | bytes 1572868
  3.6 24.3 %copy-start.8 = (f32[4]{0:T(128)S(1)}, f32[4]{0:T(128)}, u32[]{:S(2)}) copy-start(f32[4]{0:T(128)} %param.11) | copy-start | bytes 52
  6.3 32.9 %all-to-all-start = ((bf16[64,2,2048]{2,1,0:T(2,128)(2,1)}), bf16[64,2,2048]{2,1,0:T(2,128)(2,1)S(1)}, u32[]{:S(2)}, u32[]{:S(2)}) async-start(bf16[64,2,2048]{2,1,0:T(2,128)(2,1)} %reshape.374), calls=%async_computation | async-start | bytes 1048576 | tf_op jit(solution)/shard_map/all_to_all | solution.py:211
  40.8 7.9 %copy-start.2 = (bf16[4,64,1024]{2,1,0:T(8,128)(2,1)S(1)}, bf16[4,64,1024]{2,1,0:T(8,128)(2,1)}, u32[]{:S(2)}) copy-start(bf16[4,64,1024]{2,1,0:T(8,128)(2,1)} %param.10) | copy-start | bytes 1572868
  48.7 15.6 %copy-start.6 = (f32[4]{0:T(128)}, f32[4]{0:T(128)S(1)}, u32[]{:S(2)}) copy-start(f32[4]{0:T(128)S(1)} %get-tuple-element.47) | copy-start | bytes 52
  48.7 15.6 %copy-start.7 = (f32[4]{0:T(128)}, f32[4]{0:T(128)S(1)}, u32[]{:S(2)}) copy-start(f32[4]{0:T(128)S(1)} %get-tuple-element.48) | copy-start | bytes 52
  50.6 25.3 %all-to-all-start.1 = ((bf16[4,64,1024]{2,0,1:T(4,128)(2,1)}), bf16[4,64,1024]{2,0,1:T(4,128)(2,1)S(1)}, u32[]{:S(2)}, u32[]{:S(2)}) async-start(bf16[4,64,1024]{2,0,1:T(4,128)(2,1)} %fusion.64), calls=%async_computation.1 | async-start | bytes 1048576 | tf_op jit(solution)/shard_map/all_to_all | solution.py:221
  76.9 6.3 %copy-start.3 = (bf16[256,1,1024]{2,0,1:T(8,128)(2,1)S(1)}, bf16[256,1,1024]{2,0,1:T(8,128)(2,1)}, u32[]{:S(2)}) copy-start(bf16[256,1,1024]{2,0,1:T(8,128)(2,1)} %all_to_all.24) | copy-start | bytes 1572868
  76.9 6.4 %copy-start.4 = (bf16[27,128,256]{2,1,0:T(8,128)(2,1)S(1)}, bf16[27,128,256]{2,1,0:T(8,128)(2,1)}, u32[]{:S(2)}) copy-start(bf16[27,128,256]{2,1,0:T(8,128)(2,1)} %param.12) | copy-start | bytes 5308420
  79.4 15.0 %collective-permute-start = (bf16[256,1,1024]{2,0,1:T(8,128)(2,1)}, bf16[256,1,1024]{2,0,1:T(8,128)(2,1)S(1)}, u32[]{:S(2)}, u32[]{:S(2)}) collective-permute-start(bf16[256,1,1024]{2,0,1:T(8,128)(2,1)} %all_to_all.24), channel_id=1, source_target_pairs={{4,0},{8,4},{12,8},{16,12},{20,16},{24,20},{28,24},{32,28},{36,32}... | collective-permute-start | bytes 1572872 | tf_op jit(solution)/shard_map/ppermute | solution.py:169
  94.5 3.2 %collective-permute-start.1 = (bf16[256,2,64]{2,0,1:T(8,128)(2,1)S(1)}, bf16[256,2,64]{2,0,1:T(8,128)(2,1)S(1)}, u32[]{:S(2)}, u32[]{:S(2)}) collective-permute-start(bf16[256,2,64]{2,0,1:T(8,128)(2,1)S(1)} %slice.232), channel_id=1, source_target_pairs={{1,0},{2,1},{3,2},{5,4},{6,5},{7,6},{9,8},{10,9},{11,10},{13,12},{... | collective-permute-start | bytes 196616 | tf_op jit(solution)/shard_map/ppermute | solution.py:169
  124.2 4.8 %copy-start.5 = (bf16[1,1,16,1,64,1,128]{6,4,2,5,3,1,0:T(8,128)(2,1)S(1)}, bf16[1,1,16,1,64,1,128]{6,4,2,5,3,1,0:T(8,128)(2,1)}, u32[]{:S(2)}) copy-start(bf16[1,1,16,1,64,1,128]{6,4,2,5,3,1,0:T(8,128)(2,1)} %copy.91) | copy-start | bytes 786436

commit v2 on v0

v2 whole, which is shorter than its diff:
```python
import functools
import math

import jax
import jax.numpy as jnp
from jax import lax
from jax.experimental import pallas as pl
from jax.experimental.pallas import tpu as pltpu
from jax.sharding import PartitionSpec as P

MESH = pl.DeviceIdType.MESH
BF, F32 = jnp.bfloat16, jnp.float32
FIRST = 14
NT = (((1,), (1,)), ((), ()))
REACH = (((1, 0),), ((2, 0), (0, 1)))


def device(x, y, z, core):
    return (x * 16 + z * 2 + y // 2, y % 2 * 2 + core)


def remote(src, dst, send, recv, where):
    return pltpu.make_async_remote_copy(
        src_ref=src, dst_ref=dst, send_sem=send, recv_sem=recv, device_id=where, device_id_type=MESH
    )


def kernel(
    cells, scale,
    fine_hbm, og_hbm, pn_hbm, act_hbm, gain_ref, wd_hbm, wu_hbm,
    gin_hbm, down_ref, stat_ref,
    fine, og, pn, act, wd, wu, rows32, taps_up, deep32, grad8,
    a1_out, a1_in, a2_out, a2_in, h_in, pn32, act32, moment, term,
    fine_edge, f_even, f_odd, g_own, g_next, gt, gts, q, o32, gin,
    pair_out, pair_in, ax, ax_in, by, by_in, ay, ay_in, bx, bx_in, zz, zs, zs_in,
    load, a1_send, a1_recv, a2_send, a2_recv, h_send, h_recv, m_send, m_recv, t_send, t_recv,
    edge_send, edge_recv, rs_send, rs_recv, store,
):
    slab, grp = lax.axis_index("slab"), lax.axis_index("grp")
    x, y, z, core = slab // 16, slab % 2 * 2 + grp // 2, slab // 2 % 8, grp % 2
    loads = [
        pltpu.make_async_copy(src, dst, load.at[i])
        for i, (src, dst) in enumerate(
            ((og_hbm, og), (wu_hbm, wu), (fine_hbm, fine), (pn_hbm, pn), (act_hbm, act), (wd_hbm, wd))
        )
    ]
    for copy in loads:
        copy.start()
    barrier = pltpu.get_barrier_semaphore()

    def greet(d, carry):
        pl.semaphore_signal(barrier, inc=1, device_id=((slab + d) % 64, grp), device_id_type=MESH)
        return carry

    lax.fori_loop(1, 64, greet, 0)
    for d in (1, 2, 3):
        pl.semaphore_signal(barrier, inc=1, device_id=(slab, (grp + d) % 4), device_id_type=MESH)
    cross = (slab + 1 - slab % 2 * 2, (grp + 2) % 4)
    pl.semaphore_signal(barrier, inc=1, device_id=cross, device_id_type=MESH)

    low = lax.broadcasted_iota(jnp.int32, (8, 512), 0) < 4

    loads[0].wait()
    loads[1].wait()
    for side in range(4):
        taps_up[side] = jnp.concatenate([wu[2 * side], wu[2 * side + 1]], axis=1)

    def part(row, carry):
        for side in range(4):
            rows32[side] = og[side // 2, 2 * row + side % 2].astype(F32)
            at = pl.ds(pl.multiple_of(row * 64, 64), 64)
            grad8[side, at, 0:128] = rows32[side, pl.ds(0, 64, stride=2), :].astype(BF)
            grad8[side, at, 128:256] = rows32[side, pl.ds(1, 64, stride=2), :].astype(BF)
        return carry

    lax.fori_loop(0, 16, part, 0)
    total = lax.dot_general(taps_up[0], grad8[0], NT, preferred_element_type=F32)
    for side in range(1, 4):
        total = total + lax.dot_general(taps_up[side], grad8[side], NT, preferred_element_type=F32)
    deep32[...] = total

    def pieces_of(m, carry):
        at = pl.ds(pl.multiple_of(m * 8, 8), 8)
        left, right = deep32[at, 0:512], deep32[at, 512:1024]
        a1_out[2 * m] = jnp.where(low, left, pltpu.roll(right, 4, 0)).astype(BF)
        a1_out[2 * m + 1] = jnp.where(low, pltpu.roll(left, 4, 0), right).astype(BF)
        return carry

    lax.fori_loop(0, 32, pieces_of, 0)
    pl.semaphore_wait(barrier, 67)

    def a1_copy(d):
        to = (slab + d) % 64
        return remote(a1_out.at[to], a1_in.at[slab], a1_send.at[d], a1_recv.at[d], (to, grp))

    def a1_start(d, carry):
        a1_copy(d).start()
        return carry

    lax.fori_loop(1, 64, a1_start, 0)
    a1_in[slab] = a1_out[slab]

    loads[2].wait()
    edge = remote(fine.at[:, 31], fine_edge, edge_send.at[0], edge_recv.at[0], (slab, (grp + 1) % 4))
    edge.start()
    loads[3].wait()
    loads[4].wait()
    for ch in range(4):
        for half in range(2):
            for block in range(4):
                lanes = slice(half * 512 + block * 128, half * 512 + block * 128 + 128)
                pn32[block, pl.ds(half * 4 + ch, 64, stride=8), :] = pn[ch, :, lanes].astype(F32)
                act32[block, pl.ds(half * 4 + ch, 64, stride=8), :] = act[ch, :, lanes].astype(F32)

    def wide(ref, i):
        at = pl.ds(pl.multiple_of(i * 8, 8), 8)
        return jnp.concatenate([ref[block, at, :] for block in range(4)], axis=1)

    def spread(rows):
        per_row = jnp.sum(rows, axis=1, keepdims=True)
        per_row = jnp.broadcast_to(per_row, (8, 128))
        return per_row + pltpu.roll(per_row, 4, 0)

    def moments(i, carry):
        value = wide(pn32, i)
        return carry[0] + value, carry[1] + value * value

    none = jnp.zeros((8, 512), F32)
    one, two = lax.fori_loop(0, 64, moments, (none, none))
    moment[grp, 0] = spread(one)
    moment[grp, 1] = spread(two)
    m_copies = []
    for d in (1, 2, 3):
        m_copies.append(remote(moment.at[grp], moment.at[grp], m_send.at[d], m_recv.at[d], (slab, (grp + d) % 4)))
        m_copies[-1].start()

    first_row = lax.broadcasted_iota(jnp.int32, (64, 128), 0) == 0

    def place_row(slot, block, values, at):
        rows32[slot] = values.astype(F32)
        even = rows32[slot, pl.ds(0, 64, stride=2), :]
        odd = rows32[slot, pl.ds(1, 64, stride=2), :]
        block[at, 0:128] = jnp.where(first_row, 0.0, pltpu.roll(odd, 1, 0)).astype(BF)
        block[at, 128:256] = even.astype(BF)
        block[at, 256:384] = odd.astype(BF)

    def split_fine(row, carry):
        for plane in range(2):
            place_row(2 * plane, f_even.at[plane], fine[plane, 2 * row], pl.ds(pl.multiple_of(row * 64, 64), 64))
            place_row(
                2 * plane + 1, f_odd.at[plane], fine[plane, 2 * row + 1],
                pl.ds(pl.multiple_of(row * 64 + 64, 64), 64),
            )
        return carry

    lax.fori_loop(0, 16, split_fine, 0)
    edge.wait()
    for plane in range(2):
        behind = fine_edge[plane].astype(F32)
        place_row(plane, f_odd.at[plane], jnp.where(grp == 0, jnp.zeros_like(behind), behind), pl.ds(0, 64))
    for copy in m_copies:
        copy.wait()
    sums = moment[0] + moment[1] + moment[2] + moment[3]
    mean = sums[0] / cells
    inv_std = lax.rsqrt(sums[1] / cells - mean * mean + 1e-05)
    mean_w, inv_w = jnp.tile(mean, (1, 4)), jnp.tile(inv_std, (1, 4))

    def a1_wait(d, carry):
        a1_copy(d).wait()
        return carry

    lax.fori_loop(1, 64, a1_wait, 0)

    def masked_of(i):
        normed = (wide(pn32, i) - mean_w) * inv_w
        masked = jnp.where(wide(act32, i) > 0, a1_in[i].astype(F32), 0.0)
        return masked, normed

    def terms(i, carry):
        masked, normed = masked_of(i)
        return carry[0] + masked, carry[1] + masked * normed

    one, two = lax.fori_loop(0, 64, terms, (none, none))
    term[grp, 0] = spread(one)
    term[grp, 1] = spread(two)
    t_copies = []
    for d in (1, 2, 3):
        t_copies.append(remote(term.at[grp], term.at[grp], t_send.at[d], t_recv.at[d], (slab, (grp + d) % 4)))
        t_copies[-1].start()
    for copy in t_copies:
        copy.wait()
    sums = term[0] + term[1] + term[2] + term[3]
    shift, gain = sums[0] / cells, sums[1] / cells
    stat_ref[0] = gain
    stat_ref[1] = shift
    shift_w, gain_w = jnp.tile(shift, (1, 4)), jnp.tile(gain, (1, 4))
    factor_w = jnp.tile(gain_ref[...] * inv_std, (1, 4))

    def act_grad(i, carry):
        masked, normed = masked_of(i)
        a2_out[i] = (factor_w * (masked - shift_w - normed * gain_w)).astype(BF)
        return carry

    lax.fori_loop(0, 64, act_grad, 0)

    def a2_copy(d):
        to = (slab + d) % 64
        return remote(a2_out.at[to], a2_in.at[slab], a2_send.at[d], a2_recv.at[d], (to, grp))

    def a2_start(d, carry):
        a2_copy(d).start()
        return carry

    lax.fori_loop(1, 64, a2_start, 0)
    a2_in[slab] = a2_out[slab]

    def on_copy(d):
        source = (slab + 64 - d) % 64
        return remote(
            a2_in.at[source], h_in.at[source], h_send.at[d], h_recv.at[d], ((slab + 63) % 64, grp)
        )

    def a2_wait(d, carry):
        a2_copy(d).wait()
        on_copy(d).start()
        return carry

    on_copy(0).start()
    loads[5].wait()
    lax.fori_loop(1, 64, a2_wait, 0)

    def join(source, block):
        def pair_of(m):
            a, b = source[2 * m].astype(F32), source[2 * m + 1].astype(F32)
            left = jnp.where(low, a, pltpu.roll(b, 4, 0))
            right = jnp.where(low, pltpu.roll(a, 4, 0), b)
            return jnp.concatenate([left, right], axis=1)

        def step(m, carry):
            at = pl.ds(pl.multiple_of(m * 16, 16), 16)
            block[at, :] = jnp.concatenate([pair_of(2 * m), pair_of(2 * m + 1)], axis=0).astype(BF)
            return carry

        lax.fori_loop(0, 16, step, 0)

    def tap_grads(kx, block, plane):
        for ky in range(3):
            window = f_even[plane] if ky == 1 else f_odd[plane, ky * 32 : ky * 32 + 1024]
            found = jnp.dot(block[...], window, preferred_element_type=F32)
            for kz in range(3):
                q[9 * kx + 3 * ky + kz] = found[:, kz * 128 : kz * 128 + 128]

    last_cell = lax.broadcasted_iota(jnp.int32, (128, 256), 0) % 64 == 63
    last_row = lax.broadcasted_iota(jnp.int32, (64, 256), 0) == 63

    def turn(block, plane):
        for part in range(8):
            turned = jnp.transpose(block[:, part * 128 : part * 128 + 128].astype(F32))
            gt[plane, part * 128 : part * 128 + 128] = turned.astype(BF)
            moved = jnp.where(last_cell, 0.0, pltpu.roll(turned, 127, 0))
            gts[plane, part * 128 : part * 128 + 128] = moved.astype(BF)

    def edge_row(plane):
        return remote(
            gt.at[plane, 0:64], gt.at[plane, 1024:1088], edge_send.at[1 + plane], edge_recv.at[1 + plane],
            (slab, (grp + 3) % 4),
        )

    def finish_edge(plane):
        edge_row(plane).wait()
        after = gt[plane, 1024:1088].astype(F32)
        after = jnp.where(grp == 3, jnp.zeros_like(after), after)
        gt[plane, 1024:1088] = after.astype(BF)
        gts[plane, 1024:1088] = jnp.where(last_row, 0.0, pltpu.roll(after, 63, 0)).astype(BF)

    def input_grad(px, py):
        def chunk(c, carry):
            both = jnp.zeros((256, 256), F32)
            odd = jnp.zeros((256, 128), F32)
            for kx, off_x in REACH[px]:
                for ky, off_y in REACH[py]:
                    at = pl.ds(pl.multiple_of(c * 256 + off_y * 64, 64), 256)
                    tap = 9 * kx + 3 * ky
                    pair = wd[tap + 1 : tap + 3].reshape(256, 256)
                    both = both + lax.dot_general(gt[off_x, at], pair, NT, preferred_element_type=F32)
                    odd = odd + lax.dot_general(gts[off_x, at], wd[tap], NT, preferred_element_type=F32)
            o32[pl.ds(0, 256, stride=2), :] = both[:, 0:128]
            o32[pl.ds(1, 256, stride=2), :] = both[:, 128:256] + odd
            for row in range(4):
                gin[px, 8 * c + 2 * row + py] = o32[row * 128 : row * 128 + 128].astype(BF)
            return carry

        lax.fori_loop(0, 4, chunk, 0)

    join(a2_in, g_own)
    turn(g_own, 0)
    edge_row(0).start()
    tap_grads(1, g_own, 0)
    tap_grads(2, g_own, 1)
    finish_edge(0)
    input_grad(0, 0)
    input_grad(0, 1)
    gin_copies = [pltpu.make_async_copy(gin.at[px], gin_hbm.at[px], store.at[px]) for px in range(2)]
    gin_copies[0].start()

    def on_wait(d, carry):
        on_copy(d).wait()
        return carry

    lax.fori_loop(0, 64, on_wait, 0)
    join(h_in, g_next)
    ahead = g_next[...].astype(F32)
    g_next[...] = jnp.where(slab == 63, jnp.zeros_like(ahead), ahead).astype(BF)
    tap_grads(0, g_next, 1)

    def pack(tap, carry):
        for side in range(4):
            mine = q[tap, pl.ds(side * 2 + 1 - core, 32, stride=8), :]
            pair_out[tap, side] = mine.astype(BF).reshape(4, 8, 128)
        return carry

    lax.fori_loop(0, 27, pack, 0)
    pair = remote(pair_out, pair_in, rs_send.at[0], rs_recv.at[0], (slab, grp + 1 - 2 * core))
    pair.start()
    turn(g_next, 1)
    edge_row(1).start()
    pair.wait()

    def held(tap, side):
        mine = q[tap, pl.ds(side * 2 + core, 32, stride=8), :].reshape(4, 8, 128)
        return mine + pair_in[tap, side].astype(F32)

    def split_first(tap, carry):
        for side in range(4):
            found = held(tap, side).astype(BF)
            for block in range(4):
                ax[block, tap, side] = found[block]
        return carry

    def split_last(tap, carry):
        for side in range(4):
            by[side, tap] = held(tap + FIRST, side).astype(BF)
        return carry

    lax.fori_loop(0, FIRST, split_first, 0)
    wave, later, last = [], [], []
    for d in (1, 2, 3):
        to = (x + d) % 4
        wave.append(remote(ax.at[to], ax_in.at[d - 1], rs_send.at[d], rs_recv.at[d], device(to, y, z, core)))
        wave[-1].start()
    lax.fori_loop(0, 27 - FIRST, split_last, 0)
    for d in (1, 2, 3):
        to = (y + d) % 4
        wave.append(remote(by.at[to], by_in.at[d - 1], rs_send.at[3 + d], rs_recv.at[3 + d], device(x, to, z, core)))
        wave[-1].start()
    finish_edge(1)
    input_grad(1, 0)
    for copy in wave[:3]:
        copy.wait()

    def add_ax(tap, carry):
        found = ax[x, tap].astype(F32)
        for d in range(3):
            found = found + ax_in[d, tap].astype(F32)
        for block in range(4):
            ay[block, tap] = found[block]
        return carry

    lax.fori_loop(0, FIRST, add_ax, 0)
    for d in (1, 2, 3):
        to = (y + d) % 4
        later.append(remote(ay.at[to], ay_in.at[d - 1], rs_send.at[6 + d], rs_recv.at[6 + d], device(x, to, z, core)))
        later[-1].start()
    for copy in wave[3:]:
        copy.wait()

    def add_by(tap, carry):
        found = by[y, tap].astype(F32)
        for d in range(3):
            found = found + by_in[d, tap].astype(F32)
        for block in range(4):
            bx[block, tap] = found[block]
        return carry

    lax.fori_loop(0, 27 - FIRST, add_by, 0)
    for d in (1, 2, 3):
        to = (x + d) % 4
        later.append(remote(bx.at[to], bx_in.at[d - 1], rs_send.at[9 + d], rs_recv.at[9 + d], device(to, y, z, core)))
        later[-1].start()
    input_grad(1, 1)
    gin_copies[1].start()
    for copy in later:
        copy.wait()
    for tap in range(27):
        if tap < FIRST:
            found = ay[y, tap] + ay_in[0, tap] + ay_in[1, tap] + ay_in[2, tap]
        else:
            t = tap - FIRST
            found = bx[x, t] + bx_in[0, t] + bx_in[1, t] + bx_in[2, t]
        zz[tap * 8 : tap * 8 + 8, :] = found
    for row in range(8):
        zs[row] = zz[pl.ds(row, 27, stride=8), :]
    for d in range(1, 8):
        to = (z + d) % 8
        last.append(remote(zs.at[to], zs_in.at[d - 1], rs_send.at[12 + d], rs_recv.at[12 + d], device(x, y, to, core)))
        last[-1].start()
    for copy in last:
        copy.wait()
    found = zs[z]
    for d in range(7):
        found = found + zs_in[d]
    down_ref[...] = found * scale
    for copy in gin_copies:
        copy.wait()


def local(fine_input, out_grad, pre_norm, act_out, norm_gain, w_down, w_up):
    cells = pre_norm.shape[1] * pre_norm.shape[2] * lax.axis_size("grp")
    gain = jnp.broadcast_to(jnp.tile(norm_gain, 2)[:, None], (8, 128))
    rest = 27 - FIRST
    vmem = pl.BlockSpec(memory_space=pltpu.VMEM)
    anywhere = pl.BlockSpec(memory_space=pl.ANY)
    dma = pltpu.SemaphoreType.DMA
    grad_input, down, stat = pl.pallas_call(
        functools.partial(kernel, float(cells), 1.0 / math.sqrt(cells)),
        out_shape=(
            jax.ShapeDtypeStruct((2, 32, 128, 128), BF),
            jax.ShapeDtypeStruct((27, 128), F32),
            jax.ShapeDtypeStruct((2, 8, 128), F32),
        ),
        in_specs=[anywhere] * 4 + [vmem] + [anywhere] * 2,
        out_specs=(anywhere, vmem, vmem),
        scratch_shapes=[
            pltpu.VMEM((2, 32, 128, 128), BF),
            pltpu.VMEM((2, 32, 128, 128), BF),
            pltpu.VMEM((4, 64, 1024), BF),
            pltpu.VMEM((4, 64, 1024), BF),
            pltpu.VMEM((27, 128, 256), BF),
            pltpu.VMEM((8, 256, 128), BF),
            pltpu.VMEM((4, 128, 128), F32),
            pltpu.VMEM((4, 256, 256), BF),
            pltpu.VMEM((256, 1024), F32),
            pltpu.VMEM((4, 1024, 256), BF),
            pltpu.VMEM((64, 8, 512), BF),
            pltpu.VMEM((64, 8, 512), BF),
            pltpu.VMEM((64, 8, 512), BF),
            pltpu.VMEM((64, 8, 512), BF),
            pltpu.VMEM((64, 8, 512), BF),
            pltpu.VMEM((4, 512, 128), F32),
            pltpu.VMEM((4, 512, 128), F32),
            pltpu.VMEM((4, 2, 8, 128), F32),
            pltpu.VMEM((4, 2, 8, 128), F32),
            pltpu.VMEM((2, 128, 128), BF),
            pltpu.VMEM((2, 1024, 384), BF),
            pltpu.VMEM((2, 1088, 384), BF),
            pltpu.VMEM((256, 1024), BF),
            pltpu.VMEM((256, 1024), BF),
            pltpu.VMEM((2, 1088, 256), BF),
            pltpu.VMEM((2, 1088, 256), BF),
            pltpu.VMEM((27, 256, 128), F32),
            pltpu.VMEM((512, 128), F32),
            pltpu.VMEM((2, 32, 128, 128), BF),
            pltpu.VMEM((27, 4, 4, 8, 128), BF),
            pltpu.VMEM((27, 4, 4, 8, 128), BF),
            pltpu.VMEM((4, FIRST, 4, 8, 128), BF),
            pltpu.VMEM((3, FIRST, 4, 8, 128), BF),
            pltpu.VMEM((4, rest, 4, 8, 128), BF),
            pltpu.VMEM((3, rest, 4, 8, 128), BF),
            pltpu.VMEM((4, FIRST, 8, 128), F32),
            pltpu.VMEM((3, FIRST, 8, 128), F32),
            pltpu.VMEM((4, rest, 8, 128), F32),
            pltpu.VMEM((3, rest, 8, 128), F32),
            pltpu.VMEM((216, 128), F32),
            pltpu.VMEM((8, 27, 128), F32),
            pltpu.VMEM((7, 27, 128), F32),
            dma((6,)),
            dma((64,)), dma((64,)), dma((64,)), dma((64,)), dma((64,)), dma((64,)),
            dma((4,)), dma((4,)), dma((4,)), dma((4,)),
            dma((3,)), dma((3,)), dma((20,)), dma((20,)), dma((2,)),
        ],
        compiler_params=pltpu.CompilerParams(
            collective_id=0, has_side_effects=True, vmem_limit_bytes=60 * 1024 * 1024
        ),
    )(fine_input, out_grad, pre_norm, act_out, gain, w_down, w_up)
    return (grad_input, down[None], stat[0, :4, 0], stat[1, :4, 0])


def solution(mesh):
    return jax.shard_map(
        local,
        mesh=mesh,
        in_specs=(
            P("slab", "grp", None, None),
            P("slab", "grp", None, None),
            P("slab", None, "grp"),
            P("slab", None, "grp"),
            P("slab"),
            P(),
            P(),
        ),
        out_specs=(
            P("slab", "grp", None, None),
            P(("slab", "grp"), None, None),
            P("slab"),
            P("slab"),
        ),
        check_vma=False,
    )
```

time: 408 us -> 94.5 us (0.23)
  waiting for transfers between devices: 281 us -> 0 us
  Pallas kernels: 0 us -> 84.8 us
  matrix products: 39.7 us -> 0 us
  starting transfers between devices: 27.1 us -> 0 us
  local copies, waits for them, and re-layouts: 21.7 us -> 7.23 us
  between operations: 14.8 us -> 0.64 us
  blocking collectives: 11.9 us -> 0 us
  other arithmetic: 10.7 us -> 0 us
    unnamed x2 -> x0, waiting for transfers between devices: 256 us -> none
    pallas_call x0 -> x1, Pallas kernels: none -> 84.8 us  [local(): pl.pallas_call(functools.partial(kernel, float(cells), 1.0 / math.sqrt(ce...]
    dot_general x55 -> x0, matrix products: 39.7 us -> none  [the longest x27 31 us: local(): jnp.einsum('on,jo->nj', window((extended, shifted), offsets), w_down[tap_...]
    all_to_all x2 -> x0, starting transfers between devices: 21.8 us -> none  [the longest x1 14.7 us: local(): lax.all_to_all(deep_bf, 'slab', split_axis=0, concat_axis=1, tiled=True)]
    all_to_all x2 -> x0, waiting for transfers between devices: 17.8 us -> none  [the longest x1 11.2 us: local(): lax.all_to_all(deep_bf, 'slab', split_axis=0, concat_axis=1, tiled=True)]
    psum x2 -> x0, blocking collectives: 11.9 us -> none  [local(): lax.psum((first_sum, second_sum), 'grp')]
    ppermute x2 -> x0, waiting for transfers between devices: 6.97 us -> none  [from_behind(): return lax.ppermute(shard, axis, pairs)]
    ppermute x2 -> x0, starting transfers between devices: 5.26 us -> none  [from_behind(): return lax.ppermute(shard, axis, pairs)]
  transfers between devices with their start and end apart: 5 -> 0, of which waited for: 4 -> 0; matrix products, arithmetic and copies ran while one was open for 7% -> 0% of each run, Pallas kernels for 0% -> 0%
where the time goes in v2:
time: 94.5 us; the launch traced here: 92.7 us
  Pallas kernels  84.8 us (90%)
  local copies, waits for them, and re-layouts  7.23 us (8%)
    pallas_call x1, Pallas kernels, local(): pl.pallas_call(functools.partial(kernel, float(cells), 1.0 / math.sqrt(ce...  84.8 us
    unnamed x2, local copies, waits for them, and re-layouts  4.49 us

profile of v2, /device:TPU:2, one launch (start us, length us, event | category | flops | bytes accessed | tf_op | source)
XLA Modules:
  0.0 92.7 jit_solution(11077877739562590268)
XLA Ops:
  0.6 0.7 tile.2
  1.3 0.1 broadcast_in_dim.10
  1.4 0.7 broadcast_in_dim.11.gain_ref
  2.0 84.8 %shard_map.102 = (bf16[2,32,128,128]{3,2,1,0:T(8,128)(2,1)}, f32[27,128]{1,0:T(8,128)}, f32[2,8,128]{2,1,0:T(8,128)}) custom-call(bf16[2,32,128,128]{3,2,1,0:T(8,128)(2,1)} %fine_hbm.1, bf16[2,32,128,128]{3,2,1,0:T(8,128)(2,1)} %og_hbm.1, bf16[4,64,1024]{2,1,0:T(8,128)(2,1)} %pn_hbm.1, bf16[4,64,1024]{2,1,0:T(8,128)(2,1)} %act_hbm.1, ...), custom_call_target="tpu_custom_call" | custom-call | tf_op jit(solution)/shard_map/pallas_call | solution.py:424
  86.8 1.3 %slice_reduce_fusion = (f32[4]{0:T(128)}, f32[4]{0:T(128)}) fusion(f32[2,8,128]{2,1,0:T(8,128)} %get-tuple-element.9), kind=kLoop, calls=%fused_computation | loop fusion | bytes 64 | tf_op jit(solution)/shard_map/slice | solution.py:485
  88.2 1.3 %copy.12 = f32[1,27,128]{2,0,1:T(1,128)} copy(f32[1,27,128]{2,1,0:T(8,128)} %bitcast.1) | data formatting | bytes 27648
  89.5 3.2 %copy.14 = bf16[2,32,128,128]{3,2,1,0:T(8,128)(2,1)} copy(bf16[2,32,128,128]{3,2,1,0:T(8,128)(2,1)} %get-tuple-element.24) | data formatting | bytes 4194304

commit v3 on v2

--- a/solution.py
+++ b/solution.py
@@ -10,7 +10,6 @@
 
 MESH = pl.DeviceIdType.MESH
 BF, F32 = jnp.bfloat16, jnp.float32
-FIRST = 14
 NT = (((1,), (1,)), ((), ()))
 REACH = (((1, 0),), ((2, 0), (0, 1)))
 
@@ -27,21 +26,21 @@
 
 def kernel(
     cells, scale,
-    fine_hbm, og_hbm, pn_hbm, act_hbm, gain_ref, wd_hbm, wu_hbm,
-    gin_hbm, down_ref, stat_ref,
-    fine, og, pn, act, wd, wu, rows32, taps_up, deep32, grad8,
+    fine_hbm, og_hbm, pn_hbm, act_hbm, gain_hbm, wd_hbm, wu_hbm,
+    gin, down_ref, stat_ref,
+    fine, og, pn, act, wd, wu, gain_ref, rows32, taps_up, deep32, grad8,
     a1_out, a1_in, a2_out, a2_in, h_in, pn32, act32, moment, term,
-    fine_edge, f_even, f_odd, g_own, g_next, gt, gts, q, o32, gin,
+    fine_edge, f_even, f_odd, g_own, g_next, gt, gts, q, o32,
     pair_out, pair_in, ax, ax_in, by, by_in, ay, ay_in, bx, bx_in, zz, zs, zs_in,
     load, a1_send, a1_recv, a2_send, a2_recv, h_send, h_recv, m_send, m_recv, t_send, t_recv,
-    edge_send, edge_recv, rs_send, rs_recv, store,
+    edge_send, edge_recv, rs_send, rs_recv,
 ):
     slab, grp = lax.axis_index("slab"), lax.axis_index("grp")
     x, y, z, core = slab // 16, slab % 2 * 2 + grp // 2, slab // 2 % 8, grp % 2
     loads = [
         pltpu.make_async_copy(src, dst, load.at[i])
         for i, (src, dst) in enumerate(
-            ((og_hbm, og), (wu_hbm, wu), (fine_hbm, fine), (pn_hbm, pn), (act_hbm, act), (wd_hbm, wd))
+            ((og_hbm, og), (wu_hbm, wu), (fine_hbm, fine), (pn_hbm, pn), (act_hbm, act), (wd_hbm, wd), (gain_hbm, gain_ref))
         )
     ]
     for copy in loads:
@@ -105,6 +104,7 @@
     edge.start()
     loads[3].wait()
     loads[4].wait()
+    loads[6].wait()
     for ch in range(4):
         for half in range(2):
             for block in range(4):
@@ -165,12 +165,6 @@
     inv_std = lax.rsqrt(sums[1] / cells - mean * mean + 1e-05)
     mean_w, inv_w = jnp.tile(mean, (1, 4)), jnp.tile(inv_std, (1, 4))
 
-    def a1_wait(d, carry):
-        a1_copy(d).wait()
-        return carry
-
-    lax.fori_loop(1, 64, a1_wait, 0)
-
     def masked_of(i):
         normed = (wide(pn32, i) - mean_w) * inv_w
         masked = jnp.where(wide(act32, i) > 0, a1_in[i].astype(F32), 0.0)
@@ -180,7 +174,11 @@
         masked, normed = masked_of(i)
         return carry[0] + masked, carry[1] + masked * normed
 
-    one, two = lax.fori_loop(0, 64, terms, (none, none))
+    def a1_wait(d, carry):
+        a1_copy(d).wait()
+        return terms((slab + 64 - d) % 64, carry)
+
+    one, two = lax.fori_loop(1, 64, a1_wait, terms(slab, (none, none)))
     term[grp, 0] = spread(one)
     term[grp, 1] = spread(two)
     t_copies = []
@@ -194,24 +192,29 @@
     stat_ref[0] = gain
     stat_ref[1] = shift
     shift_w, gain_w = jnp.tile(shift, (1, 4)), jnp.tile(gain, (1, 4))
-    factor_w = jnp.tile(gain_ref[...] * inv_std, (1, 4))
-
-    def act_grad(i, carry):
+    channel = lax.broadcasted_iota(jnp.int32, (8, 128), 0) % 4
+    norm_gain = jnp.full((8, 128), gain_ref[0], F32)
+    for ch in range(1, 4):
+        norm_gain = jnp.where(channel == ch, gain_ref[ch], norm_gain)
+    factor_w = jnp.tile(norm_gain * inv_std, (1, 4))
+
+    def act_grad(i):
         masked, normed = masked_of(i)
         a2_out[i] = (factor_w * (masked - shift_w - normed * gain_w)).astype(BF)
-        return carry
-
-    lax.fori_loop(0, 64, act_grad, 0)
 
     def a2_copy(d):
         to = (slab + d) % 64
         return remote(a2_out.at[to], a2_in.at[slab], a2_send.at[d], a2_recv.at[d], (to, grp))
 
     def a2_start(d, carry):
-        a2_copy(d).start()
-        return carry
-
-    lax.fori_loop(1, 64, a2_start, 0)
+        act_grad((slab + d) % 64)
+        a2_copy(d - 1).start()
+        return carry
+
+    act_grad((slab + 1) % 64)
+    lax.fori_loop(2, 64, a2_start, 0)
+    act_grad(slab)
+    a2_copy(63).start()
     a2_in[slab] = a2_out[slab]
 
     def on_copy(d):
@@ -273,7 +276,7 @@
         gt[plane, 1024:1088] = after.astype(BF)
         gts[plane, 1024:1088] = jnp.where(last_row, 0.0, pltpu.roll(after, 63, 0)).astype(BF)
 
-    def input_grad(px, py):
+    def input_grad(px, py, begin=0, end=4):
         def chunk(c, carry):
             both = jnp.zeros((256, 256), F32)
             odd = jnp.zeros((256, 128), F32)
@@ -290,18 +293,71 @@
                 gin[px, 8 * c + 2 * row + py] = o32[row * 128 : row * 128 + 128].astype(BF)
             return carry
 
-        lax.fori_loop(0, 4, chunk, 0)
+        lax.fori_loop(begin, end, chunk, 0)
+
+    def pack(first, slot):
+        def step(i, carry):
+            for side in range(4):
+                found = q[first + i, pl.ds(side * 2 + 1 - core, 32, stride=8), :]
+                pair_out[slot + i, side] = found.astype(BF).reshape(4, 8, 128)
+            return carry
+
+        lax.fori_loop(0, 9, step, 0)
+
+    def pair_copy(part):
+        at = pl.ds(part * 9, 9)
+        return remote(
+            pair_out.at[at], pair_in.at[at], rs_send.at[part], rs_recv.at[part], (slab, grp + 1 - 2 * core)
+        )
+
+    def held(tap, slot, side):
+        found = q[tap, pl.ds(side * 2 + core, 32, stride=8), :].reshape(4, 8, 128)
+        return found + pair_in[slot, side].astype(F32)
+
+    def ax_copy(part, d):
+        to, i, at = (x + d) % 4, 2 + part * 3 + d, pl.ds(part * 9, 9)
+        return remote(ax.at[to, at], ax_in.at[d - 1, at], rs_send.at[i], rs_recv.at[i], device(to, y, z, core))
+
+    def by_copy(d):
+        to, i = (y + d) % 4, 8 + d
+        return remote(by.at[to], by_in.at[d - 1], rs_send.at[i], rs_recv.at[i], device(x, to, z, core))
+
+    def ay_copy(d):
+        to, i = (y + d) % 4, 11 + d
+        return remote(ay.at[to], ay_in.at[d - 1], rs_send.at[i], rs_recv.at[i], device(x, to, z, core))
+
+    def bx_copy(d):
+        to, i = (x + d) % 4, 14 + d
+        return remote(bx.at[to], bx_in.at[d - 1], rs_send.at[i], rs_recv.at[i], device(to, y, z, core))
+
+    def split_x(part):
+        def step(i, carry):
+            slot = part * 9 + i
+            for side in range(4):
+                found = held(9 + slot, slot, side).astype(BF)
+                for block in range(4):
+                    ax[block, slot, side] = found[block]
+            return carry
+
+        lax.fori_loop(0, 9, step, 0)
 
     join(a2_in, g_own)
+    tap_grads(1, g_own, 0)
+    pack(9, 0)
+    pair_copy(0).start()
+    tap_grads(2, g_own, 1)
+    pack(18, 9)
+    pair_copy(1).start()
     turn(g_own, 0)
     edge_row(0).start()
-    tap_grads(1, g_own, 0)
-    tap_grads(2, g_own, 1)
+    for part in range(2):
+        pair_copy(part).wait()
+        split_x(part)
+        for d in (1, 2, 3):
+            ax_copy(part, d).start()
     finish_edge(0)
     input_grad(0, 0)
     input_grad(0, 1)
-    gin_copies = [pltpu.make_async_copy(gin.at[px], gin_hbm.at[px], store.at[px]) for px in range(2)]
-    gin_copies[0].start()
 
     def on_wait(d, carry):
         on_copy(d).wait()
@@ -312,124 +368,113 @@
     ahead = g_next[...].astype(F32)
     g_next[...] = jnp.where(slab == 63, jnp.zeros_like(ahead), ahead).astype(BF)
     tap_grads(0, g_next, 1)
-
-    def pack(tap, carry):
-        for side in range(4):
-            mine = q[tap, pl.ds(side * 2 + 1 - core, 32, stride=8), :]
-            pair_out[tap, side] = mine.astype(BF).reshape(4, 8, 128)
-        return carry
-
-    lax.fori_loop(0, 27, pack, 0)
-    pair = remote(pair_out, pair_in, rs_send.at[0], rs_recv.at[0], (slab, grp + 1 - 2 * core))
-    pair.start()
+    pack(0, 18)
+    pair_copy(2).start()
     turn(g_next, 1)
     edge_row(1).start()
-    pair.wait()
-
-    def held(tap, side):
-        mine = q[tap, pl.ds(side * 2 + core, 32, stride=8), :].reshape(4, 8, 128)
-        return mine + pair_in[tap, side].astype(F32)
-
-    def split_first(tap, carry):
+    pair_copy(2).wait()
+
+    def split_y(i, carry):
         for side in range(4):
-            found = held(tap, side).astype(BF)
-            for block in range(4):
-                ax[block, tap, side] = found[block]
-        return carry
-
-    def split_last(tap, carry):
-        for side in range(4):
-            by[side, tap] = held(tap + FIRST, side).astype(BF)
-        return carry
-
-    lax.fori_loop(0, FIRST, split_first, 0)
-    wave, later, last = [], [], []
-    for d in (1, 2, 3):
-        to = (x + d) % 4
-        wave.append(remote(ax.at[to], ax_in.at[d - 1], rs_send.at[d], rs_recv.at[d], device(to, y, z, core)))
-        wave[-1].start()
-    lax.fori_loop(0, 27 - FIRST, split_last, 0)
-    for d in (1, 2, 3):
-        to = (y + d) % 4
-        wave.append(remote(by.at[to], by_in.at[d - 1], rs_send.at[3 + d], rs_recv.at[3 + d], device(x, to, z, core)))
-        wave[-1].start()
+            by[side, i] = held(i, 18 + i, side).astype(BF)
+        return carry
+
+    lax.fori_loop(0, 9, split_y, 0)
+    for d in (1, 2, 3):
+        by_copy(d).start()
+    for part in range(2):
+        for d in (1, 2, 3):
+            ax_copy(part, d).wait()
+
+    def add_x(slot, carry):
+        found = ax[x, slot].astype(F32)
+        for d in range(3):
+            found = found + ax_in[d, slot].astype(F32)
+        for block in range(4):
+            ay[block, slot] = found[block]
+        return carry
+
+    lax.fori_loop(0, 18, add_x, 0)
+    for d in (1, 2, 3):
+        ay_copy(d).start()
     finish_edge(1)
     input_grad(1, 0)
-    for copy in wave[:3]:
-        copy.wait()
-
-    def add_ax(tap, carry):
-        found = ax[x, tap].astype(F32)
+    for d in (1, 2, 3):
+        by_copy(d).wait()
+
+    def add_y(i, carry):
+        found = by[y, i].astype(F32)
         for d in range(3):
-            found = found + ax_in[d, tap].astype(F32)
+            found = found + by_in[d, i].astype(F32)
         for block in range(4):
-            ay[block, tap] = found[block]
-        return carry
-
-    lax.fori_loop(0, FIRST, add_ax, 0)
-    for d in (1, 2, 3):
-        to = (y + d) % 4
-        later.append(remote(ay.at[to], ay_in.at[d - 1], rs_send.at[6 + d], rs_recv.at[6 + d], device(x, to, z, core)))
-        later[-1].start()
-    for copy in wave[3:]:
-        copy.wait()
-
-    def add_by(tap, carry):
-        found = by[y, tap].astype(F32)
-        for d in range(3):
-            found = found + by_in[d, tap].astype(F32)
-        for block in range(4):
-            bx[block, tap] = found[block]
-        return carry
-
-    lax.fori_loop(0, 27 - FIRST, add_by, 0)
-    for d in (1, 2, 3):
-        to = (x + d) % 4
-        later.append(remote(bx.at[to], bx_in.at[d - 1], rs_send.at[9 + d], rs_recv.at[9 + d], device(to, y, z, core)))
-        later[-1].start()
-    input_grad(1, 1)
-    gin_copies[1].start()
-    for copy in later:
-        copy.wait()
+            bx[block, i] = found[block]
+        return carry
+
+    lax.fori_loop(0, 9, add_y, 0)
+    for d in (1, 2, 3):
+        bx_copy(d).start()
+    input_grad(1, 1, 0, 2)
+    for d in (1, 2, 3):
+        ay_copy(d).wait()
+        bx_copy(d).wait()
     for tap in range(27):
-        if tap < FIRST:
-            found = ay[y, tap] + ay_in[0, tap] + ay_in[1, tap] + ay_in[2, tap]
+        if tap < 9:
+            found = bx[x, tap] + bx_in[0, tap] + bx_in[1, tap] + bx_in[2, tap]
         else:
-            t = tap - FIRST
-            found = bx[x, t] + bx_in[0, t] + bx_in[1, t] + bx_in[2, t]
+            t = tap - 9
+            found = ay[y, t] + ay_in[0, t] + ay_in[1, t] + ay_in[2, t]
         zz[tap * 8 : tap * 8 + 8, :] = found
     for row in range(8):
         zs[row] = zz[pl.ds(row, 27, stride=8), :]
+    def z_copy(d):
+        to, i = (z + d) % 8, 17 + d
+        return remote(zs.at[to], zs_in.at[d - 1], rs_send.at[i], rs_recv.at[i], device(x, y, to, core))
+
     for d in range(1, 8):
-        to = (z + d) % 8
-        last.append(remote(zs.at[to], zs_in.at[d - 1], rs_send.at[12 + d], rs_recv.at[12 + d], device(x, y, to, core)))
-        last[-1].start()
-    for copy in last:
-        copy.wait()
+        z_copy(d).start()
+    input_grad(1, 1, 2, 4)
+    for d in range(1, 8):
+        z_copy(d).wait()
     found = zs[z]
     for d in range(7):
         found = found + zs_in[d]
-    down_ref[...] = found * scale
-    for copy in gin_copies:
+    for tap in range(27):
+        down_ref[tap] = found[tap : tap + 1] * scale
+
+
+def write(gin, down, stat, gin_out, down_out, gain_out, shift_out, sem):
+    copies = [
+        pltpu.make_async_copy(gin, gin_out, sem.at[0]),
+        pltpu.make_async_copy(down, down_out, sem.at[1]),
+    ]
+    for copy in copies:
+        copy.start()
+    row = lax.broadcasted_iota(jnp.int32, (8, 128), 0)
+    lane = lax.broadcasted_iota(jnp.int32, (8, 128), 1)
+    for ch in range(4):
+        here = (row == ch) & (lane == 0)
+        gain_out[ch] = jnp.sum(jnp.where(here, stat[0], 0.0))
+        shift_out[ch] = jnp.sum(jnp.where(here, stat[1], 0.0))
+    for copy in copies:
         copy.wait()
 
 
 def local(fine_input, out_grad, pre_norm, act_out, norm_gain, w_down, w_up):
     cells = pre_norm.shape[1] * pre_norm.shape[2] * lax.axis_size("grp")
-    gain = jnp.broadcast_to(jnp.tile(norm_gain, 2)[:, None], (8, 128))
-    rest = 27 - FIRST
+    arrays = (fine_input, out_grad, pre_norm, act_out, norm_gain, w_down, w_up)
     vmem = pl.BlockSpec(memory_space=pltpu.VMEM)
-    anywhere = pl.BlockSpec(memory_space=pl.ANY)
+    smem = pl.BlockSpec(memory_space=pltpu.SMEM)
+    hbm = pl.BlockSpec(memory_space=pltpu.HBM)
     dma = pltpu.SemaphoreType.DMA
     grad_input, down, stat = pl.pallas_call(
         functools.partial(kernel, float(cells), 1.0 / math.sqrt(cells)),
         out_shape=(
             jax.ShapeDtypeStruct((2, 32, 128, 128), BF),
-            jax.ShapeDtypeStruct((27, 128), F32),
+            jax.ShapeDtypeStruct((27, 1, 128), F32),
             jax.ShapeDtypeStruct((2, 8, 128), F32),
         ),
-        in_specs=[anywhere] * 4 + [vmem] + [anywhere] * 2,
-        out_specs=(anywhere, vmem, vmem),
+        in_specs=[hbm] * 7,
+        out_specs=(vmem, vmem, vmem),
         scratch_shapes=[
             pltpu.VMEM((2, 32, 128, 128), BF),
             pltpu.VMEM((2, 32, 128, 128), BF),
@@ -437,6 +482,7 @@
             pltpu.VMEM((4, 64, 1024), BF),
             pltpu.VMEM((27, 128, 256), BF),
             pltpu.VMEM((8, 256, 128), BF),
+            pltpu.SMEM((4,), F32),
             pltpu.VMEM((4, 128, 128), F32),
             pltpu.VMEM((4, 256, 256), BF),
             pltpu.VMEM((256, 1024), F32),
@@ -459,30 +505,42 @@
             pltpu.VMEM((2, 1088, 256), BF),
             pltpu.VMEM((27, 256, 128), F32),
             pltpu.VMEM((512, 128), F32),
-            pltpu.VMEM((2, 32, 128, 128), BF),
             pltpu.VMEM((27, 4, 4, 8, 128), BF),
             pltpu.VMEM((27, 4, 4, 8, 128), BF),
-            pltpu.VMEM((4, FIRST, 4, 8, 128), BF),
-            pltpu.VMEM((3, FIRST, 4, 8, 128), BF),
-            pltpu.VMEM((4, rest, 4, 8, 128), BF),
-            pltpu.VMEM((3, rest, 4, 8, 128), BF),
-            pltpu.VMEM((4, FIRST, 8, 128), F32),
-            pltpu.VMEM((3, FIRST, 8, 128), F32),
-            pltpu.VMEM((4, rest, 8, 128), F32),
-            pltpu.VMEM((3, rest, 8, 128), F32),
+            pltpu.VMEM((4, 18, 4, 8, 128), BF),
+            pltpu.VMEM((3, 18, 4, 8, 128), BF),
+            pltpu.VMEM((4, 9, 4, 8, 128), BF),
+            pltpu.VMEM((3, 9, 4, 8, 128), BF),
+            pltpu.VMEM((4, 18, 8, 128), F32),
+            pltpu.VMEM((3, 18, 8, 128), F32),
+            pltpu.VMEM((4, 9, 8, 128), F32),
+            pltpu.VMEM((3, 9, 8, 128), F32),
             pltpu.VMEM((216, 128), F32),
             pltpu.VMEM((8, 27, 128), F32),
             pltpu.VMEM((7, 27, 128), F32),
-            dma((6,)),
+            dma((7,)),
             dma((64,)), dma((64,)), dma((64,)), dma((64,)), dma((64,)), dma((64,)),
             dma((4,)), dma((4,)), dma((4,)), dma((4,)),
-            dma((3,)), dma((3,)), dma((20,)), dma((20,)), dma((2,)),
+            dma((3,)), dma((3,)), dma((25,)), dma((25,)),
         ],
         compiler_params=pltpu.CompilerParams(
-            collective_id=0, has_side_effects=True, vmem_limit_bytes=60 * 1024 * 1024
+            collective_id=0, has_side_effects=True, vmem_limit_bytes=40 * 1024 * 1024
         ),
-    )(fine_input, out_grad, pre_norm, act_out, gain, w_down, w_up)
-    return (grad_input, down[None], stat[0, :4, 0], stat[1, :4, 0])
+    )(*[pltpu.with_memory_space_constraint(array, pltpu.HBM) for array in arrays])
+    grad_input, down, gain, shift = pl.pallas_call(
+        write,
+        out_shape=(
+            jax.ShapeDtypeStruct((2, 32, 128, 128), BF),
+            jax.ShapeDtypeStruct((27, 1, 128), F32),
+            jax.ShapeDtypeStruct((4,), F32),
+            jax.ShapeDtypeStruct((4,), F32),
+        ),
+        in_specs=[vmem] * 3,
+        out_specs=(hbm, hbm, smem, smem),
+        scratch_shapes=[dma((2,))],
+        compiler_params=pltpu.CompilerParams(vmem_limit_bytes=2 * 1024 * 1024),
+    )(grad_input, down, stat)
+    return (grad_input, down.transpose(1, 0, 2), gain, shift)
 
 
 def solution(mesh):

time: 94.5 us -> 83.4 us (0.88)
  local copies, waits for them, and re-layouts: 7.23 us -> 0 us
  Pallas kernels: 84.8 us -> 81.8 us
    pallas_call x1, Pallas kernels: 84.8 us -> 80 us  [local(): pl.pallas_call(functools.partial(kernel, float(cells), 1.0 / math.sqrt(ce...]
    unnamed x2 -> x0, local copies, waits for them, and re-layouts: 4.49 us -> none
    pallas_call x0 -> x1, Pallas kernels: none -> 1.87 us  [local(): pl.pallas_call(write, out_shape=(jax.ShapeDtypeStruct((2, 32, 128, 128),...]
    slice x1 -> x0, local copies, waits for them, and re-layouts: 1.34 us -> none  [local(): return (grad_input, down[None], stat[0, :4, 0], stat[1, :4, 0])]
where the time goes in v3:
time: 83.4 us; the launch traced here: 82.5 us
  Pallas kernels  81.8 us (98%)
    pallas_call x1, Pallas kernels, local(): pl.pallas_call(functools.partial(kernel, float(cells), 1.0 / math.sqrt(ce...  80 us
    pallas_call x1, Pallas kernels, local(): pl.pallas_call(write, out_shape=(jax.ShapeDtypeStruct((2, 32, 128, 128),...  1.87 us

profile of v3, /device:TPU:2, one launch (start us, length us, event | category | flops | bytes accessed | tf_op | source)
XLA Modules:
  0.0 82.5 jit_solution(3762465559263712434)
XLA Ops:
  0.6 80.0 %shard_map.102 = (bf16[2,32,128,128]{3,2,1,0:T(8,128)(2,1)S(1)}, f32[27,1,128]{2,1,0:T(1,128)S(1)}, f32[2,8,128]{2,1,0:T(8,128)S(1)}) custom-call(bf16[2,32,128,128]{3,2,1,0:T(8,128)(2,1)} %fine_hbm.1, bf16[2,32,128,128]{3,2,1,0:T(8,128)(2,1)} %og_hbm.1, bf16[4,64,1024]{2,1,0:T(8,128)(2,1)} %pn_hbm.1, bf16[4,64,1024]{2,1,0:T(8,128)(2,1)} %act_hbm.1, ...), custom_call_target="tpu_custom_call" | custom-call | tf_op jit(solution)/shard_map/pallas_call | solution.py:469
  80.6 1.9 %shard_map.103 = (bf16[2,32,128,128]{3,2,1,0:T(8,128)(2,1)}, f32[27,1,128]{2,1,0:T(1,128)}, f32[4]{0:T(128)}, f32[4]{0:T(128)}) custom-call(bf16[2,32,128,128]{3,2,1,0:T(8,128)(2,1)S(1)} %get-tuple-element.11.gin, f32[27,1,128]{2,1,0:T(1,128)S(1)} %get-tuple-element.12.down, f32[2,8,128]{2,1,0:T(8,128)S(1)} %get-tuple-element.13.stat), custom_call_target="tpu_custom_call" | custom-call | tf_op jit(solution)/shard_map/pallas_call | solution.py:530

commit v4 on v3

--- a/solution.py
+++ b/solution.py
@@ -31,7 +31,7 @@
     fine, og, pn, act, wd, wu, gain_ref, rows32, taps_up, deep32, grad8,
     a1_out, a1_in, a2_out, a2_in, h_in, pn32, act32, moment, term,
     fine_edge, f_even, f_odd, g_own, g_next, gt, gts, q, o32,
-    pair_out, pair_in, ax, ax_in, by, by_in, ay, ay_in, bx, bx_in, zz, zs, zs_in,
+    pair_out, pair_in, ax, ax_in, by, by_in, ay, ay_in, ay_own, zz, zs, zs_in,
     load, a1_send, a1_recv, a2_send, a2_recv, h_send, h_recv, m_send, m_recv, t_send, t_recv,
     edge_send, edge_recv, rs_send, rs_recv,
 ):
@@ -54,8 +54,9 @@
     lax.fori_loop(1, 64, greet, 0)
     for d in (1, 2, 3):
         pl.semaphore_signal(barrier, inc=1, device_id=(slab, (grp + d) % 4), device_id_type=MESH)
-    cross = (slab + 1 - slab % 2 * 2, (grp + 2) % 4)
-    pl.semaphore_signal(barrier, inc=1, device_id=cross, device_id_type=MESH)
+    for d in range(1, 8):
+        cross = ((x + d // 2) % 4 * 16 + z * 2 + (slab + d) % 2, (grp + 2) % 4)
+        pl.semaphore_signal(barrier, inc=1, device_id=cross, device_id_type=MESH)
 
     low = lax.broadcasted_iota(jnp.int32, (8, 512), 0) < 4
 
@@ -86,10 +87,16 @@
         return carry
 
     lax.fori_loop(0, 32, pieces_of, 0)
-    pl.semaphore_wait(barrier, 67)
+    pl.semaphore_wait(barrier, 73)
+
+    def target(d):
+        return (slab + d) % 64
+
+    def origin(d):
+        return (slab + 64 - d) % 64
 
     def a1_copy(d):
-        to = (slab + d) % 64
+        to = target(d)
         return remote(a1_out.at[to], a1_in.at[slab], a1_send.at[d], a1_recv.at[d], (to, grp))
 
     def a1_start(d, carry):
@@ -176,7 +183,7 @@
 
     def a1_wait(d, carry):
         a1_copy(d).wait()
-        return terms((slab + 64 - d) % 64, carry)
+        return terms(origin(d), carry)
 
     one, two = lax.fori_loop(1, 64, a1_wait, terms(slab, (none, none)))
     term[grp, 0] = spread(one)
@@ -203,22 +210,22 @@
         a2_out[i] = (factor_w * (masked - shift_w - normed * gain_w)).astype(BF)
 
     def a2_copy(d):
-        to = (slab + d) % 64
+        to = target(d)
         return remote(a2_out.at[to], a2_in.at[slab], a2_send.at[d], a2_recv.at[d], (to, grp))
 
     def a2_start(d, carry):
-        act_grad((slab + d) % 64)
+        act_grad(target(d))
         a2_copy(d - 1).start()
         return carry
 
-    act_grad((slab + 1) % 64)
+    act_grad(target(1))
     lax.fori_loop(2, 64, a2_start, 0)
     act_grad(slab)
     a2_copy(63).start()
     a2_in[slab] = a2_out[slab]
 
     def on_copy(d):
-        source = (slab + 64 - d) % 64
+        source = origin(d)
         return remote(
             a2_in.at[source], h_in.at[source], h_send.at[d], h_recv.at[d], ((slab + 63) % 64, grp)
         )
@@ -232,7 +239,7 @@
     loads[5].wait()
     lax.fori_loop(1, 64, a2_wait, 0)
 
-    def join(source, block):
+    def join(source, block, keep=None):
         def pair_of(m):
             a, b = source[2 * m].astype(F32), source[2 * m + 1].astype(F32)
             left = jnp.where(low, a, pltpu.roll(b, 4, 0))
@@ -241,13 +248,16 @@
 
         def step(m, carry):
             at = pl.ds(pl.multiple_of(m * 16, 16), 16)
-            block[at, :] = jnp.concatenate([pair_of(2 * m), pair_of(2 * m + 1)], axis=0).astype(BF)
+            found = jnp.concatenate([pair_of(2 * m), pair_of(2 * m + 1)], axis=0)
+            if keep is not None:
+                found = jnp.where(keep, found, jnp.zeros_like(found))
+            block[at, :] = found.astype(BF)
             return carry
 
         lax.fori_loop(0, 16, step, 0)
 
-    def tap_grads(kx, block, plane):
-        for ky in range(3):
+    def tap_grads(kx, block, plane, rows=(0, 1, 2)):
+        for ky in rows:
             window = f_even[plane] if ky == 1 else f_odd[plane, ky * 32 : ky * 32 + 1024]
             found = jnp.dot(block[...], window, preferred_element_type=F32)
             for kz in range(3):
@@ -295,17 +305,17 @@
 
         lax.fori_loop(begin, end, chunk, 0)
 
-    def pack(first, slot):
+    def pack(first, slot, count=9):
         def step(i, carry):
             for side in range(4):
                 found = q[first + i, pl.ds(side * 2 + 1 - core, 32, stride=8), :]
                 pair_out[slot + i, side] = found.astype(BF).reshape(4, 8, 128)
             return carry
 
-        lax.fori_loop(0, 9, step, 0)
-
-    def pair_copy(part):
-        at = pl.ds(part * 9, 9)
+        lax.fori_loop(0, count, step, 0)
+
+    def pair_copy(part, slot, count):
+        at = pl.ds(slot, count)
         return remote(
             pair_out.at[at], pair_in.at[at], rs_send.at[part], rs_recv.at[part], (slab, grp + 1 - 2 * core)
         )
@@ -315,20 +325,27 @@
         return found + pair_in[slot, side].astype(F32)
 
     def ax_copy(part, d):
-        to, i, at = (x + d) % 4, 2 + part * 3 + d, pl.ds(part * 9, 9)
+        to, i, at = (x + d) % 4, 4 + part * 3 + d, pl.ds(part * 9, 9)
         return remote(ax.at[to, at], ax_in.at[d - 1, at], rs_send.at[i], rs_recv.at[i], device(to, y, z, core))
 
+    def ay_copy(part, d):
+        to, i, at = (y + d) % 4, 10 + part * 18 + d, pl.ds(part * 9, 9)
+        return remote(ay.at[to, at], ay_in.at[d - 1, at], rs_send.at[i], rs_recv.at[i], device(x, to, z, core))
+
     def by_copy(d):
-        to, i = (y + d) % 4, 8 + d
-        return remote(by.at[to], by_in.at[d - 1], rs_send.at[i], rs_recv.at[i], device(x, to, z, core))
-
-    def ay_copy(d):
-        to, i = (y + d) % 4, 11 + d
-        return remote(ay.at[to], ay_in.at[d - 1], rs_send.at[i], rs_recv.at[i], device(x, to, z, core))
-
-    def bx_copy(d):
-        to, i = (x + d) % 4, 14 + d
-        return remote(bx.at[to], bx_in.at[d - 1], rs_send.at[i], rs_recv.at[i], device(to, y, z, core))
+        to_x, to_y, i = (x + d // 4) % 4, (y + d % 4) % 4, 13 + d
+        return remote(
+            by.at[to_x * 4 + to_y], by_in.at[d - 1], rs_send.at[i], rs_recv.at[i], device(to_x, to_y, z, core)
+        )
+
+    def add_x(slot, carry):
+        found = ax[x, slot].astype(F32)
+        for d in range(3):
+            found = found + ax_in[d, slot].astype(F32)
+        ay_own[slot] = found
+        for block in range(4):
+            ay[block, slot] = found[block].astype(BF)
+        return carry
 
     def split_x(part):
         def step(i, carry):
@@ -344,19 +361,31 @@
     join(a2_in, g_own)
     tap_grads(1, g_own, 0)
     pack(9, 0)
-    pair_copy(0).start()
+    pair_copy(0, 0, 9).start()
     tap_grads(2, g_own, 1)
     pack(18, 9)
-    pair_copy(1).start()
-    turn(g_own, 0)
-    edge_row(0).start()
-    for part in range(2):
-        pair_copy(part).wait()
+    pair_copy(1, 9, 9).start()
+
+    def first_wave(part):
+        pair_copy(part, part * 9, 9).wait()
         split_x(part)
         for d in (1, 2, 3):
             ax_copy(part, d).start()
+
+    def second_wave(part):
+        for d in (1, 2, 3):
+            ax_copy(part, d).wait()
+        lax.fori_loop(part * 9, part * 9 + 9, add_x, 0)
+        for d in (1, 2, 3):
+            ay_copy(part, d).start()
+
+    first_wave(0)
+    turn(g_own, 0)
+    edge_row(0).start()
+    first_wave(1)
     finish_edge(0)
     input_grad(0, 0)
+    second_wave(0)
     input_grad(0, 1)
 
     def on_wait(d, carry):
@@ -364,70 +393,51 @@
         return carry
 
     lax.fori_loop(0, 64, on_wait, 0)
-    join(h_in, g_next)
-    ahead = g_next[...].astype(F32)
-    g_next[...] = jnp.where(slab == 63, jnp.zeros_like(ahead), ahead).astype(BF)
-    tap_grads(0, g_next, 1)
-    pack(0, 18)
-    pair_copy(2).start()
+    join(h_in, g_next, slab != 63)
+    for ky in range(3):
+        tap_grads(0, g_next, 1, (ky,))
+        pack(3 * ky, 18 + 3 * ky, 3)
+        pair_copy(2 + ky, 18 + 3 * ky, 3).start()
     turn(g_next, 1)
     edge_row(1).start()
-    pair_copy(2).wait()
 
     def split_y(i, carry):
         for side in range(4):
-            by[side, i] = held(i, 18 + i, side).astype(BF)
-        return carry
-
-    lax.fori_loop(0, 9, split_y, 0)
-    for d in (1, 2, 3):
+            found = held(i, 18 + i, side).astype(BF)
+            for block in range(4):
+                by[block * 4 + side, i] = found[block]
+        return carry
+
+    for ky in range(3):
+        pair_copy(2 + ky, 18 + 3 * ky, 3).wait()
+        lax.fori_loop(3 * ky, 3 * ky + 3, split_y, 0)
+    for d in range(1, 16):
         by_copy(d).start()
+    second_wave(1)
+    finish_edge(1)
+    input_grad(1, 0)
+    input_grad(1, 1, 0, 2)
     for part in range(2):
         for d in (1, 2, 3):
-            ax_copy(part, d).wait()
-
-    def add_x(slot, carry):
-        found = ax[x, slot].astype(F32)
-        for d in range(3):
-            found = found + ax_in[d, slot].astype(F32)
-        for block in range(4):
-            ay[block, slot] = found[block]
-        return carry
-
-    lax.fori_loop(0, 18, add_x, 0)
-    for d in (1, 2, 3):
-        ay_copy(d).start()
-    finish_edge(1)
-    input_grad(1, 0)
-    for d in (1, 2, 3):
+            ay_copy(part, d).wait()
+    for d in range(1, 16):
         by_copy(d).wait()
-
-    def add_y(i, carry):
-        found = by[y, i].astype(F32)
-        for d in range(3):
-            found = found + by_in[d, i].astype(F32)
-        for block in range(4):
-            bx[block, i] = found[block]
-        return carry
-
-    lax.fori_loop(0, 9, add_y, 0)
-    for d in (1, 2, 3):
-        bx_copy(d).start()
-    input_grad(1, 1, 0, 2)
-    for d in (1, 2, 3):
-        ay_copy(d).wait()
-        bx_copy(d).wait()
+    own = x * 4 + y
     for tap in range(27):
         if tap < 9:
-            found = bx[x, tap] + bx_in[0, tap] + bx_in[1, tap] + bx_in[2, tap]
+            found = by[own, tap].astype(F32)
+            for d in range(15):
+                found = found + by_in[d, tap].astype(F32)
         else:
             t = tap - 9
-            found = ay[y, t] + ay_in[0, t] + ay_in[1, t] + ay_in[2, t]
+            found = ay_own[t, y]
+            for d in range(3):
+                found = found + ay_in[d, t].astype(F32)
         zz[tap * 8 : tap * 8 + 8, :] = found
     for row in range(8):
-        zs[row] = zz[pl.ds(row, 27, stride=8), :]
+        zs[row] = zz[pl.ds(row, 27, stride=8), :].astype(BF)
     def z_copy(d):
-        to, i = (z + d) % 8, 17 + d
+        to, i = (z + d) % 8, 31 + d
         return remote(zs.at[to], zs_in.at[d - 1], rs_send.at[i], rs_recv.at[i], device(x, y, to, core))
 
     for d in range(1, 8):
@@ -435,9 +445,9 @@
     input_grad(1, 1, 2, 4)
     for d in range(1, 8):
         z_copy(d).wait()
-    found = zs[z]
+    found = zz[pl.ds(z, 27, stride=8), :]
     for d in range(7):
-        found = found + zs_in[d]
+        found = found + zs_in[d].astype(F32)
     for tap in range(27):
         down_ref[tap] = found[tap : tap + 1] * scale
 
@@ -509,19 +519,18 @@
             pltpu.VMEM((27, 4, 4, 8, 128), BF),
             pltpu.VMEM((4, 18, 4, 8, 128), BF),
             pltpu.VMEM((3, 18, 4, 8, 128), BF),
-            pltpu.VMEM((4, 9, 4, 8, 128), BF),
-            pltpu.VMEM((3, 9, 4, 8, 128), BF),
-            pltpu.VMEM((4, 18, 8, 128), F32),
-            pltpu.VMEM((3, 18, 8, 128), F32),
-            pltpu.VMEM((4, 9, 8, 128), F32),
-            pltpu.VMEM((3, 9, 8, 128), F32),
+            pltpu.VMEM((16, 9, 8, 128), BF),
+            pltpu.VMEM((15, 9, 8, 128), BF),
+            pltpu.VMEM((4, 18, 8, 128), BF),
+            pltpu.VMEM((3, 18, 8, 128), BF),
+            pltpu.VMEM((18, 4, 8, 128), F32),
             pltpu.VMEM((216, 128), F32),
-            pltpu.VMEM((8, 27, 128), F32),
-            pltpu.VMEM((7, 27, 128), F32),
+            pltpu.VMEM((8, 27, 128), BF),
+            pltpu.VMEM((7, 27, 128), BF),
             dma((7,)),
             dma((64,)), dma((64,)), dma((64,)), dma((64,)), dma((64,)), dma((64,)),
             dma((4,)), dma((4,)), dma((4,)), dma((4,)),
-            dma((3,)), dma((3,)), dma((25,)), dma((25,)),
+            dma((3,)), dma((3,)), dma((40,)), dma((40,)),
         ],
         compiler_params=pltpu.CompilerParams(
             collective_id=0, has_side_effects=True, vmem_limit_bytes=40 * 1024 * 1024

time: 83.4 us -> 79.7 us (0.956)
  Pallas kernels: 81.8 us -> 77.9 us
    pallas_call x1, Pallas kernels: 80 us -> 76 us  [local(): pl.pallas_call(functools.partial(kernel, float(cells), 1.0 / math.sqrt(ce...]
where the time goes in v4:
time: 79.7 us; the launch traced here: 78.5 us
  Pallas kernels  77.9 us (98%)
    pallas_call x1, Pallas kernels, local(): pl.pallas_call(functools.partial(kernel, float(cells), 1.0 / math.sqrt(ce...  76 us
    pallas_call x1, Pallas kernels, local(): pl.pallas_call(write, out_shape=(jax.ShapeDtypeStruct((2, 32, 128, 128),...  1.87 us

profile of v4, /device:TPU:2, one launch (start us, length us, event | category | flops | bytes accessed | tf_op | source)
XLA Modules:
  0.0 78.5 jit_solution(12874189254154816319)
XLA Ops:
  0.6 76.0 %shard_map.102 = (bf16[2,32,128,128]{3,2,1,0:T(8,128)(2,1)S(1)}, f32[27,1,128]{2,1,0:T(1,128)S(1)}, f32[2,8,128]{2,1,0:T(8,128)S(1)}) custom-call(bf16[2,32,128,128]{3,2,1,0:T(8,128)(2,1)} %fine_hbm.1, bf16[2,32,128,128]{3,2,1,0:T(8,128)(2,1)} %og_hbm.1, bf16[4,64,1024]{2,1,0:T(8,128)(2,1)} %pn_hbm.1, bf16[4,64,1024]{2,1,0:T(8,128)(2,1)} %act_hbm.1, ...), custom_call_target="tpu_custom_call" | custom-call | tf_op jit(solution)/shard_map/pallas_call | solution.py:479
  76.7 1.9 %shard_map.103 = (bf16[2,32,128,128]{3,2,1,0:T(8,128)(2,1)}, f32[27,1,128]{2,1,0:T(1,128)}, f32[4]{0:T(128)}, f32[4]{0:T(128)}) custom-call(bf16[2,32,128,128]{3,2,1,0:T(8,128)(2,1)S(1)} %get-tuple-element.11.gin, f32[27,1,128]{2,1,0:T(1,128)S(1)} %get-tuple-element.12.down, f32[2,8,128]{2,1,0:T(8,128)S(1)} %get-tuple-element.13.stat), custom_call_target="tpu_custom_call" | custom-call | tf_op jit(solution)/shard_map/pallas_call | solution.py:539

commit v5 on v4

--- a/solution.py
+++ b/solution.py
@@ -384,9 +384,7 @@
     edge_row(0).start()
     first_wave(1)
     finish_edge(0)
-    input_grad(0, 0)
     second_wave(0)
-    input_grad(0, 1)
 
     def on_wait(d, carry):
         on_copy(d).wait()
@@ -415,8 +413,9 @@
         by_copy(d).start()
     second_wave(1)
     finish_edge(1)
+    input_grad(0, 0)
+    input_grad(0, 1)
     input_grad(1, 0)
-    input_grad(1, 1, 0, 2)
     for part in range(2):
         for d in (1, 2, 3):
             ay_copy(part, d).wait()
@@ -442,7 +441,7 @@
 
     for d in range(1, 8):
         z_copy(d).start()
-    input_grad(1, 1, 2, 4)
+    input_grad(1, 1)
     for d in range(1, 8):
         z_copy(d).wait()
     found = zz[pl.ds(z, 27, stride=8), :]

time: 79.7 us -> 78.1 us (0.980)
  Pallas kernels: 77.9 us -> 76.4 us
    pallas_call x1, Pallas kernels: 76 us -> 74.6 us  [local(): pl.pallas_call(functools.partial(kernel, float(cells), 1.0 / math.sqrt(ce...]
where the time goes in v5:
time: 78.1 us; the launch traced here: 77.1 us
  Pallas kernels  76.4 us (98%)
    pallas_call x1, Pallas kernels, local(): pl.pallas_call(functools.partial(kernel, float(cells), 1.0 / math.sqrt(ce...  74.6 us
    pallas_call x1, Pallas kernels, local(): pl.pallas_call(write, out_shape=(jax.ShapeDtypeStruct((2, 32, 128, 128),...  1.87 us

profile of v5, /device:TPU:2, one launch (start us, length us, event | category | flops | bytes accessed | tf_op | source)
XLA Modules:
  0.0 77.1 jit_solution(1341273164374255019)
XLA Ops:
  0.6 74.6 %shard_map.102 = (bf16[2,32,128,128]{3,2,1,0:T(8,128)(2,1)S(1)}, f32[27,1,128]{2,1,0:T(1,128)S(1)}, f32[2,8,128]{2,1,0:T(8,128)S(1)}) custom-call(bf16[2,32,128,128]{3,2,1,0:T(8,128)(2,1)} %fine_hbm.1, bf16[2,32,128,128]{3,2,1,0:T(8,128)(2,1)} %og_hbm.1, bf16[4,64,1024]{2,1,0:T(8,128)(2,1)} %pn_hbm.1, bf16[4,64,1024]{2,1,0:T(8,128)(2,1)} %act_hbm.1, ...), custom_call_target="tpu_custom_call" | custom-call | tf_op jit(solution)/shard_map/pallas_call | solution.py:478
  75.2 1.9 %shard_map.103 = (bf16[2,32,128,128]{3,2,1,0:T(8,128)(2,1)}, f32[27,1,128]{2,1,0:T(1,128)}, f32[4]{0:T(128)}, f32[4]{0:T(128)}) custom-call(bf16[2,32,128,128]{3,2,1,0:T(8,128)(2,1)S(1)} %get-tuple-element.11.gin, f32[27,1,128]{2,1,0:T(1,128)S(1)} %get-tuple-element.12.down, f32[2,8,128]{2,1,0:T(8,128)S(1)} %get-tuple-element.13.stat), custom_call_target="tpu_custom_call" | custom-call | tf_op jit(solution)/shard_map/pallas_call | solution.py:538
